TPU v7x, 256 devices: a whole 4x4x8 slice. The times are simulated.
256 devices in a mesh: seq: 64 (over x, z, core), head: 4 (over y).
Axes of the slice: x: 4, y: 4, z: 8, core: 2. Of those that a mesh axis runs over, the one named last changes fastest.
Arguments:
- values: float32 [16384, 2560], P('seq', 'head'), may hold values from -6 to 6
- input_map: float32 [16384, 128], P('seq'), may hold values from -6 to 6
- output_map: float32 [16384, 128], P('seq'), may hold values from -6 to 6
- step_sizes: float32 [40, 16384], P('head', 'seq'), may hold values from 0.004 to 0.02
- decay_rates: float32 [40], P('head'), may hold values from 0.02 to 2
- skip_gains: float32 [40], P('head'), may hold values from 0.5 to 1.5
- doc_lengths: int32 [128], replicated, may hold values from 1 to 1024, 16384 in all
- out_grad: float32 [16384, 2560], P('seq', 'head'), may hold values from -6 to 6
Outputs:
- outputs: bfloat16 [16384, 2560], P('seq', 'head')
- grad_values: bfloat16 [16384, 2560], P('seq', 'head')
- grad_input_map: float32 [16384, 128], P('seq')
- grad_output_map: float32 [16384, 128], P('seq')
Inputs may be any that keep to these rules, and one draw needn't show every extreme that they name: `doc_lengths`: the documents fill the stream of 16384 tokens in order; no document has more than 1024 tokens, and one has exactly that many.
All inputs are finite; a program needn't handle non-finite values.
Results may differ from a plain program's by a relative error of at most 0.001.
Values sent between devices are 32-bit elements; how exact they have to be, the bound alone decides.
No kernel may reach another device: no remote copies, remote signals or barrier semaphores. Data moves between devices by JAX's collectives and lax.ppermute only.
A program may use at most 128 MiB of HBM per device.

v0:
```python
import jax
import jax.numpy as jnp
from jax import lax
from jax.sharding import PartitionSpec as P

HEAD_SIZE = 64
GROUP = 256


highest = lax.Precision.HIGHEST


def entering_2(part, axis, combine, identity, reverse):
    count = lax.axis_size(axis)
    place = lax.axis_index(axis)
    ahead = count - 1 - place if reverse else place
    gathered = jax.tree.map(lambda a: lax.all_gather(a, axis), part)
    state = jax.tree.map(lambda a, e: jnp.zeros_like(a) + jnp.asarray(e, a.dtype), part, identity)

    def one(hop, state):
        source = count - 1 - hop if reverse else hop
        return combine(
            state, jax.tree.map(lambda a: lax.dynamic_index_in_dim(a, source, 0, False), gathered)
        )

    return lax.fori_loop(0, ahead, one, state)


def edge_decays(log_decay, restart):
    running = jnp.cumsum(log_decay, axis=1)
    resets_seen = jnp.cumsum(restart)
    inward = jnp.where(resets_seen[None, :] == 0, jnp.exp(running), 0.0)
    outward = jnp.where(
        resets_seen[None, :] == resets_seen[-1], jnp.exp(running[:, -1:] - running), 0.0
    )
    whole_decay = jnp.where(resets_seen[-1] == 0, jnp.exp(running[:, -1]), 0.0)
    return (running, resets_seen, inward, outward, whole_decay)


def group_pass(values, bmat, cmat, steps, rates, skips, restart, grad_y):
    length, head_count, head_width = values.shape
    blocks = length // GROUP
    log_decay = -rates[:, None] * steps

    def blocked(array):
        return array.reshape((blocks, GROUP) + array.shape[1:])

    def blocked_heads(array):
        return jnp.transpose(array.reshape(head_count, blocks, GROUP), (1, 0, 2))

    grouped = (
        blocked(values),
        blocked(grad_y),
        blocked(bmat),
        blocked(cmat),
        blocked_heads(steps),
        blocked_heads(log_decay),
        blocked(restart),
    )
    causal = jnp.arange(GROUP)[:, None] >= jnp.arange(GROUP)[None, :]

    def forward(carry_state, item):
        piece_x, piece_g, piece_b, piece_c, piece_dt, piece_log, piece_reset = item
        running, resets_seen, inward, outward, whole_decay = edge_decays(piece_log, piece_reset)
        visible = causal & (resets_seen[:, None] == resets_seen[None, :])
        inner = jnp.where(
            visible[None], jnp.exp(jnp.minimum(running[:, :, None] - running[:, None, :], 0.0)), 0.0
        )
        scaled = piece_x * piece_dt.T[:, :, None]
        scores = jnp.dot(piece_c, piece_b.T, precision=highest)
        mixing = inner * scores[None]
        entering = inward.T[:, :, None]
        result = jnp.einsum("hts,shp->thp", mixing, scaled, precision=highest)
        result = result + entering * jnp.einsum(
            "tn,hpn->thp", piece_c, carry_state, precision=highest
        )
        result = result + skips[None, :, None] * piece_x
        products = jnp.einsum("thp,shp->hts", piece_g, piece_x, precision=highest)
        weight = inner * products * piece_dt[:, None, :]
        grad_x = (
            jnp.einsum("hts,thp->shp", mixing, piece_g, precision=highest) * piece_dt.T[:, :, None]
        )
        grad_x = grad_x + skips[None, :, None] * piece_g
        grad_b = jnp.einsum("hts,tn->sn", weight, piece_c, precision=highest)
        grad_c = jnp.einsum("hts,sn->tn", weight, piece_b, precision=highest)
        grad_c = grad_c + jnp.einsum(
            "hpn,thp->tn", carry_state, piece_g * entering, precision=highest
        )
        updated = whole_decay[:, None, None] * carry_state + jnp.einsum(
            "shp,sn->hpn", scaled * outward.T[:, :, None], piece_b, precision=highest
        )
        return (updated, (result, grad_x, grad_b, grad_c, inward, outward, whole_decay))

    zeros_state = jnp.zeros((head_count, head_width, bmat.shape[1]), jnp.float32)
    end_state, outs = lax.scan(forward, zeros_state, grouped)
    result, grad_x, grad_b, grad_c, inwards, outwards, wholes = outs

    def backward(carry_grad, item):
        piece_x, piece_g, piece_b, piece_c, piece_dt, inward, outward, whole_decay = item
        factor = (piece_dt * outward).T[:, :, None]
        extra_x = factor * jnp.einsum("hpn,sn->shp", carry_grad, piece_b, precision=highest)
        extra_b = jnp.einsum("hpn,shp->sn", carry_grad, piece_x * factor, precision=highest)
        earlier_grad = whole_decay[:, None, None] * carry_grad + jnp.einsum(
            "thp,tn->hpn", piece_g * inward.T[:, :, None], piece_c, precision=highest
        )
        return (earlier_grad, (extra_x, extra_b))

    start_grad, (extra_x, extra_b) = lax.scan(
        backward,
        zeros_state,
        (grouped[0], grouped[1], grouped[2], grouped[3], grouped[4], inwards, outwards, wholes),
        reverse=True,
    )
    result = result.reshape(length, head_count, head_width)
    grad_x = (grad_x + extra_x).reshape(length, head_count, head_width)
    grad_b = (grad_b + extra_b).reshape(length, -1)
    grad_c = grad_c.reshape(length, -1)
    return (result, grad_x, grad_b, grad_c, end_state, start_grad)


def combine_pair(earlier, later_part):
    return (earlier[0] * later_part[0], later_part[0][:, None, None] * earlier[1] + later_part[1])


def body(values, input_map, output_map, step_sizes, decay_rates, skip_gains, doc_lengths, out_grad):
    length = values.shape[0]
    head_count = values.shape[1] // HEAD_SIZE
    shaped_x = values.reshape(length, head_count, HEAD_SIZE)
    shaped_g = out_grad.reshape(length, head_count, HEAD_SIZE)
    positions = lax.axis_index("seq") * length + jnp.arange(length, dtype=jnp.int32)
    starts = jnp.cumsum(doc_lengths) - doc_lengths
    restart = jnp.any(starts[:, None] == positions[None, :], axis=0).astype(jnp.float32)
    result, grad_x, grad_b, grad_c, end_state, start_grad = group_pass(
        shaped_x, input_map, output_map, step_sizes, decay_rates, skip_gains, restart, shaped_g
    )
    running, resets_seen, inward, outward, whole_decay = edge_decays(
        -decay_rates[:, None] * step_sizes, restart
    )
    identity = (jnp.ones_like(whole_decay), jnp.zeros_like(end_state))
    state_in = entering_2((whole_decay, end_state), "seq", combine_pair, identity, False)[1]
    grad_after = entering_2((whole_decay, start_grad), "seq", combine_pair, identity, True)[1]
    entering = inward.T[:, :, None]
    result = result + entering * jnp.einsum("tn,hpn->thp", output_map, state_in, precision=highest)
    grad_c = grad_c + jnp.einsum("hpn,thp->tn", state_in, shaped_g * entering, precision=highest)
    factor = (step_sizes * outward).T[:, :, None]
    grad_x = grad_x + factor * jnp.einsum("hpn,sn->shp", grad_after, input_map, precision=highest)
    grad_b = grad_b + jnp.einsum("hpn,shp->sn", grad_after, shaped_x * factor, precision=highest)
    grad_b, grad_c = lax.psum((grad_b, grad_c), "head")
    return (
        result.reshape(length, -1).astype(jnp.bfloat16),
        grad_x.reshape(length, -1).astype(jnp.bfloat16),
        grad_b,
        grad_c,
    )


def solution(mesh):
    placed = (
        P("seq", "head"),
        P("seq", None),
        P("seq", None),
        P("head", "seq"),
        P("head"),
        P("head"),
        P(),
        P("seq", "head"),
    )
    return jax.shard_map(
        body,
        mesh=mesh,
        in_specs=placed,
        out_specs=(P("seq", "head"), P("seq", "head"), P("seq", None), P("seq", None)),
        check_vma=False,
    )
```

profile of v0, /device:TPU:6, one launch (start us, length us, event | category | flops | bytes accessed | tf_op | source)
XLA Modules:
  0.0 415.3 jit_solution(13744933926897372859)
XLA Ops:
  14.2 1.3 copy.36
  16.4 2.3 convolution_add_fusion.1
  19.2 1.4 convolution_add_fusion
  22.2 112.2 %all-reduce = f32[640]{0:T(1024)S(1)} all-reduce(f32[640]{0:T(1024)S(1)} %dynamic-update-slice), channel_id=2, replica_groups=mesh['seq'=64,'head'=4] {'seq'}, use_global_device_ids=true, to_apply=%add | all-reduce | flops 640 | bytes 5120
  135.1 1.9 convolution_bitcast_fusion.7
  137.0 1.9 convolution_bitcast_fusion.5
  140.1 2.5 fusion.27
  143.3 3.0 multiply_reduce_fusion
  146.4 87.4 %while.16 = (s32[]{:T(128)}, f32[10,64,128]{2,1,0:T(8,128)S(1)}, s32[]{:T(128)}, f32[64,10]{1,0:T(8,128)}, f32[64,10,64,128]{3,2,1,0:T(8,128)}, /*index=5*/s32[]{:T(128)}, s32[]{:T(128)}, s32[]{:T(128)}) while((s32[]{:T(128)}, f32[10,64,128]{2,1,0:T(8,128)S(1)}, s32[]{:T(128)}, f32[64,10]{1,0:T(8,128)}, f32[64,10,64,128]{3,2,1,0:T(8,128)}, ...), condition=%wide.region_7.8_spmd, body=%wide.region_6.7_spmd.sunk | while | flops 163845 | bytes 983287 | solution.py:26
  149.0 1.1 bitcast_add_fusion.4
  152.6 1.1 bitcast_add_fusion.4
  156.2 1.1 bitcast_add_fusion.4
  159.9 1.1 bitcast_add_fusion.4
  163.5 1.1 bitcast_add_fusion.4
  165.3 1.1 bitcast_add_fusion.4
  167.1 1.1 bitcast_add_fusion.4
  168.9 1.1 bitcast_add_fusion.4
  170.8 1.1 bitcast_add_fusion.4
  185.3 1.1 bitcast_add_fusion.4
  190.7 1.1 bitcast_add_fusion.4
  192.5 1.1 bitcast_add_fusion.4
  194.4 1.1 bitcast_add_fusion.4
  198.1 1.1 bitcast_add_fusion.4
  201.7 1.1 bitcast_add_fusion.4
  203.6 1.1 bitcast_add_fusion.4
  209.0 1.1 bitcast_add_fusion.4
  210.8 1.1 bitcast_add_fusion.4
  212.6 1.1 bitcast_add_fusion.4
  216.3 1.1 bitcast_add_fusion.4
  218.1 1.1 bitcast_add_fusion.4
  220.0 1.1 bitcast_add_fusion.4
  221.8 1.1 bitcast_add_fusion.4
  223.6 1.1 bitcast_add_fusion.4
  225.4 1.1 bitcast_add_fusion.4
  227.2 1.1 bitcast_add_fusion.4
  229.1 1.1 bitcast_add_fusion.4
  230.9 1.1 bitcast_add_fusion.4
  232.7 1.1 bitcast_add_fusion.4
  233.8 1.9 convolution_bitcast_fusion.4
  235.7 1.5 fusion.40
  237.2 4.8 %all-gather.8.cloned.1.call-done = f32[640,64,128]{2,1,0:T(8,128)} async-done(((f32[10,64,128]{2,1,0:T(8,128)}), f32[640,64,128]{2,1,0:T(8,128)}) %all-gather.8.cloned.1.call-update) | async-done | bytes 20971536 | tf_op jit(solution)/shard_map/all_gather | solution.py:17
  242.0 27.4 %while.17 = (s32[]{:T(128)}, f32[10,64,128]{2,1,0:T(8,128)S(1)}, s32[]{:T(128)}, f32[64,10]{1,0:T(8,128)}, f32[64,10,64,128]{3,2,1,0:T(8,128)}, /*index=5*/s32[]{:T(128)}, s32[]{:T(128)}, s32[]{:T(128)}, s32[]{:T(128)}) while((s32[]{:T(128)}, f32[10,64,128]{2,1,0:T(8,128)S(1)}, s32[]{:T(128)}, f32[64,10]{1,0:T(8,128)}, ...), condition=%wide.region_9.10_spmd, body=%wide.region_8.9_spmd.sunk | while | flops 163846 | bytes 983307 | solution.py:26
  269.4 1.9 convolution_bitcast_fusion.6
  272.9 2.2 fusion.47
  276.2 4.3 %fusion.43 = bf16[256,10,64]{0,2,1:T(8,128)(2,1)S(1)} fusion(f32[256,10,64]{0,2,1:T(8,128)} %fusion.40, f32[256,10,64]{0,2,1:T(8,128)S(1)} %fusion.41, f32[256,256]{1,0:T(8,128)} %copy-done.6, f32[10,256]{1,0:T(8,128)} %bitcast.138, pred[256,256]{1,0:T(8,128)(4,1)} %copy-done.9, f32[256,10,64]{0,2,1:T(8,128)S(1)} %bitcast.121, f32[10]{0:T(128)} %param.17, ...), kind=kOutput, calls=%fused_computation.37 | convolution fusion | flops 506920960 | bytes 2641960 | tf_op jit(solution)/shard_map/while/body/eval_jaxpr/hts,shp->thp/dot_general | solution.py:73
  281.4 124.3 %all-reduce.4.cloned.1.call-done = (f32[256,128]{1,0:T(8,128)}, f32[256,128]{1,0:T(8,128)}) async-done(((f32[256,128]{1,0:T(8,128)}, f32[256,128]{1,0:T(8,128)}), (f32[256,128]{1,0:T(8,128)}, f32[256,128]{1,0:T(8,128)})) %all-reduce.4.cloned.1.call-update) | async-done | bytes 262160 | tf_op jit(solution)/shard_map/psum | solution.py:148
  405.7 1.6 copy.66
  407.2 1.6 copy.67
  (173 shorter events, 95.4 us)
Async XLA Ops:
  7.2 12.0 %copy-start = (f32[256,128]{1,0:T(8,128)S(1)}, f32[256,128]{1,0:T(8,128)}, u32[]{:S(2)}) copy-start(f32[256,128]{1,0:T(8,128)} %param.14) | copy-start | bytes 393220
  7.2 11.6 %copy-start.2 = (f32[256,640]{1,0:T(8,128)S(1)}, f32[256,640]{1,0:T(8,128)}, u32[]{:S(2)}) copy-start(f32[256,640]{1,0:T(8,128)} %param.19) | copy-start | bytes 1966084
  7.2 139.2 %all-gather.6.cloned.1.call-start = ((), (), s32[]{:S(2)}) async-start(), calls=%async_computation | async-start | bytes 21299200 | tf_op jit(solution)/shard_map/all_gather | solution.py:17
  14.0 129.3 %copy-start.8 = (f32[2,8,2,128]{3,1,2,0:T(8,128)}, f32[2,8,2,128]{3,1,2,0:T(8,128)S(1)}, u32[]{:S(2)}) copy-start(f32[2,8,2,128]{3,1,2,0:T(8,128)S(1)} %copy.44) | copy-start | bytes 49156
  16.4 4.3 %copy-start.11 = (u32[256]{0:T(256)S(1)}, u32[256]{0:T(256)}, u32[]{:S(2)}) copy-start(u32[256]{0:T(256)} %constant.132) | copy-start | bytes 3076
  18.8 120.3 %copy-start.1 = (f32[256,128]{1,0:T(8,128)S(1)}, f32[256,128]{1,0:T(8,128)}, u32[]{:S(2)}) copy-start(f32[256,128]{1,0:T(8,128)} %param.13) | copy-start | bytes 393220
  18.8 223.2 %all-gather.8.cloned.1.call-start = ((), (), s32[]{:S(2)}) async-start(), calls=%async_computation.1 | async-start | bytes 21299200 | tf_op jit(solution)/shard_map/all_gather | solution.py:17
  19.1 121.1 %copy-start.7 = (f32[10,256]{1,0:T(8,128)S(1)}, f32[10,256]{1,0:T(8,128)}, u32[]{:S(2)}) copy-start(f32[10,256]{1,0:T(8,128)} %param.15) | copy-start | bytes 30724
  19.1 121.1 %copy-start.10 = (f32[10]{0:T(128)S(1)}, f32[10]{0:T(128)}, u32[]{:S(2)}) copy-start(f32[10]{0:T(128)} %param.17) | copy-start | bytes 124
  20.6 385.1 %all-reduce.4.cloned.1.call-start = ((), (), s32[]{:S(2)}) async-start(), calls=%async_computation.2 | async-start | bytes 524288 | tf_op jit(solution)/shard_map/psum | solution.py:148
  139.0 4.3 %copy-start.9 = (pred[256,256]{1,0:T(8,128)(4,1)}, pred[256,256]{1,0:T(8,128)(4,1)S(1)}, u32[]{:S(2)}) copy-start(pred[256,256]{1,0:T(8,128)(4,1)S(1)} %fusion.62) | copy-start | bytes 196612
  139.4 3.2 copy-start.6
  269.4 3.5 copy-start.4
  269.4 5.7 %copy-start.3 = (f32[256,128]{1,0:T(8,128)S(1)}, f32[256,128]{1,0:T(8,128)}, u32[]{:S(2)}) copy-start(f32[256,128]{1,0:T(8,128)} %convolution_bitcast_fusion.5) | copy-start | bytes 393220
  269.4 5.7 %copy-start.5 = (f32[256,128]{1,0:T(8,128)S(1)}, f32[256,128]{1,0:T(8,128)}, u32[]{:S(2)}) copy-start(f32[256,128]{1,0:T(8,128)} %convolution_bitcast_fusion.4) | copy-start | bytes 393220
Sparse Core Ops, SparseCore 0:
  18.9 112.0 all-gather.5
  134.3 107.6 all-gather.7
  276.3 129.3 all-reduce.3
where the time goes:
time: 420 us; the launch traced here: 415 us
  waiting for transfers between devices  129 us (31%)
  blocking collectives  112 us (27%)
  other arithmetic  74.1 us (18%)
  local copies, waits for them, and re-layouts  53.9 us (13%)
  matrix products  28.2 us (7%)
  between operations  15.4 us (4%)
    psum x1, waiting for transfers between devices, body(): grad_b, grad_c = lax.psum((grad_b, grad_c), 'head')  124 us
    unnamed x1, blocking collectives  112 us
    add x63, other arithmetic, combine_pair(): later_part[0][:, None, None] * earlier[1] + later_part[1]  68.7 us
    mul x63, local copies, waits for them, and re-layouts, combine_pair(): later_part[0][:, None, None] * earlier[1] + later_part[1]  43.9 us
  transfers between devices with their start and end apart: 3, of which 2 were waited for; matrix products, arithmetic and copies ran while one was open for 26% of the time, Pallas kernels for 0%

commit v1 on v0

v1 whole, which is shorter than its diff:
```python
import jax
import jax.numpy as jnp
from jax import lax
from jax.experimental import pallas as pl
from jax.experimental.pallas import tpu as pltpu
from jax.sharding import PartitionSpec as P

HEAD_SIZE = 64
STATE = 128
f32 = jnp.float32
bf16 = jnp.bfloat16

NN = (((1,), (0,)), ((), ()))
NT = (((1,), (1,)), ((), ()))


def halves(a):
    high = a.astype(bf16)
    return high, (a - high.astype(f32)).astype(bf16)


def thirds(a):
    high = a.astype(bf16)
    rest = a - high.astype(f32)
    mid = rest.astype(bf16)
    return high, mid, (rest - mid.astype(f32)).astype(bf16)


def dot(a, b, dims):
    return lax.dot_general(a, b, dims, preferred_element_type=f32)


def dot3(a, b, dims):
    return dot(a[0], b[0], dims) + (dot(a[0], b[1], dims) + dot(a[1], b[0], dims))


def spread(cols, heads, width):
    row = lax.broadcasted_iota(jnp.int32, (3 * heads, width), 0)
    lane = lax.broadcasted_iota(jnp.int32, (3 * heads, width), 1)
    first = (row - jnp.where(row >= heads, heads, 0) - jnp.where(row >= 2 * heads, heads, 0)) * HEAD_SIZE
    pick = ((lane >= first) & (lane < first + HEAD_SIZE)).astype(f32).astype(bf16)
    parts = jnp.concatenate([p.astype(f32) for p in thirds(cols)], axis=1).astype(bf16)
    return dot(parts, pick, NN)


def segments(docs, first, length):
    count = docs.shape[1]
    up = lax.broadcasted_iota(jnp.int32, (count, count), 0)
    across = lax.broadcasted_iota(jnp.int32, (count, count), 1)
    start_col = jnp.sum(jnp.where(across < up, docs, 0.0), axis=1, keepdims=True)
    docs_col = jnp.sum(jnp.where(across == up, docs, 0.0), axis=1, keepdims=True)
    start_row = jnp.sum(jnp.where(up < across, docs_col, 0.0), axis=0, keepdims=True)
    at_col = (lax.broadcasted_iota(jnp.int32, (length, 1), 0) + first).astype(f32)
    at_row = (lax.broadcasted_iota(jnp.int32, (1, length), 1) + first).astype(f32)
    seg_col = jnp.sum(jnp.where(start_row <= at_col, 1.0, 0.0), axis=1, keepdims=True)
    seg_row = jnp.sum(jnp.where(start_col <= at_row, 1.0, 0.0), axis=0, keepdims=True)
    before = jnp.sum(jnp.where(start_row < first.astype(f32), 1.0, 0.0), axis=1, keepdims=True)
    return seg_col, seg_row, before


def head_row(ref, heads, width):
    lane = lax.broadcasted_iota(jnp.int32, (1, width), 1)
    out = jnp.zeros((1, width), f32)
    for h in range(heads):
        out = jnp.where((lane >= h * HEAD_SIZE) & (lane < (h + 1) * HEAD_SIZE), ref[h], out)
    return out


def edge_kernel(place, rates, docs, dt, x, g, b, c, send, keep, xh, xl, gh, gl, facts, segs, segr, last):
    length, width = x.shape
    heads = dt.shape[0]
    core = place[0] % 2
    first = place[0] * length
    seg_col, seg_row, before = segments(docs[...].astype(f32), first, length)
    seg_last = seg_col[length - 1 :, :]
    entry = (seg_col == before).astype(f32)
    final = (seg_col == seg_last).astype(f32)
    through = (seg_last == before).astype(f32)

    rate_col = jnp.zeros((heads, 1), f32)
    which = lax.broadcasted_iota(jnp.int32, (heads, 1), 0)
    for h in range(heads):
        rate_col = jnp.where(which == h, rates[h], rate_col)
    steps = dt[...]
    logs = -rate_col * steps
    t_at = lax.broadcasted_iota(jnp.int32, (length, length), 0)
    s_at = lax.broadcasted_iota(jnp.int32, (length, length), 1)
    lower = (s_at <= t_at).astype(f32).astype(bf16)
    eye = (s_at == t_at).astype(f32).astype(bf16)
    run = sum(dot(lower, p, NT) for p in thirds(logs))
    steps_t = sum(dot(eye, p, NT) for p in thirds(steps))
    grow = jnp.exp(run)
    shrink = jnp.exp(-run) * steps_t
    facts[...] = jnp.concatenate([grow, shrink], axis=1)
    col = lax.broadcasted_iota(jnp.int32, (length, 8), 1)
    segs[...] = jnp.where(col == 0, seg_col, jnp.where(col == 1, entry, final))
    segr[...] = jnp.broadcast_to(seg_row, (8, length))

    grow_x = spread(grow, heads, width)
    shrink_x = spread(shrink, heads, width)
    total = grow_x[length - 1 :, :]
    x_parts = halves(x[...] * shrink_x)
    g_parts = halves(g[...] * grow_x)
    xh[...], xl[...] = x_parts
    gh[...], gl[...] = g_parts
    b_parts = halves((b[...] * final).T)
    c_parts = halves((c[...] * entry).T)
    end = dot3(b_parts, x_parts, NN) * total
    start = dot3(c_parts, g_parts, NN)
    last[...] = jnp.broadcast_to(total, (8, width))
    whole = jnp.broadcast_to(total * through, (8, width))
    is_zero = core == 0
    send[:STATE, :] = jnp.where(is_zero, start, end)
    keep[:STATE, :] = jnp.where(is_zero, end, start)
    send[STATE:, :] = whole
    keep[STATE:, :] = whole


def local_kernel(skips, facts, segs, segr, x, g, xh, xl, gh, gl, b, c, y0, z0, grads):
    length, width = x.shape
    heads = facts.shape[1] // 2
    b_parts = halves(b[...])
    c_parts = halves(c[...])
    t_at = lax.broadcasted_iota(jnp.int32, (length, length), 0)
    s_at = lax.broadcasted_iota(jnp.int32, (length, length), 1)
    same = segs[:, :1] == segr[:1, :]
    mask = jnp.where(same & (s_at <= t_at), 1.0, 0.0)
    mask_t = jnp.where(same & (t_at <= s_at), 1.0, 0.0)
    x_parts = (xh[...], xl[...])
    g_parts = (gh[...], gl[...])
    mix = halves(dot3(c_parts, b_parts, NT) * mask)
    mix_t = halves(dot3(b_parts, c_parts, NT) * mask_t)
    skip = head_row(skips, heads, width)
    y0[...] = dot3(mix, x_parts, NN) * spread(facts[:, :heads], heads, width) + skip * x[...]
    z0[...] = dot3(mix_t, g_parts, NN) * spread(facts[:, heads:], heads, width) + skip * g[...]
    weight = dot3(g_parts, x_parts, NT) * mask
    grads[:length, :] = dot3(halves(weight.T), c_parts, NN)
    grads[length:, :] = dot3(halves(weight), b_parts, NN)


def grad_kernel(place, mine, other, last, segs, xh, xl, gh, gl, grads, total):
    length, width = xh.shape
    is_zero = place[0] % 2 == 0
    mine_, other_ = mine[...], other[...]
    into = jnp.where(is_zero, mine_, other_)
    after = jnp.where(is_zero, other_, mine_) * last[:1, :]
    grad_b = dot3((xh[...], xl[...]), halves(after), NT) * segs[:, 2:3]
    grad_c = dot3((gh[...], gl[...]), halves(into), NT) * segs[:, 1:2]
    total[:length, :] = grads[:length, :] + grad_b
    total[length:, :] = grads[length:, :] + grad_c


def out_kernel(place, mine, other, last, facts, segs, b, c, y0, z0, y, z):
    length, width = y0.shape
    heads = facts.shape[1] // 2
    is_zero = place[0] % 2 == 0
    mine_, other_ = mine[...], other[...]
    into = halves(jnp.where(is_zero, mine_, other_))
    after = halves(jnp.where(is_zero, other_, mine_) * last[:1, :])
    c_parts = halves(c[...] * segs[:, 1:2])
    b_parts = halves(b[...] * segs[:, 2:3])
    y[...] = (y0[...] + dot3(c_parts, into, NN) * spread(facts[:, :heads], heads, width)).astype(bf16)
    z[...] = (z0[...] + dot3(b_parts, after, NN) * spread(facts[:, heads:], heads, width)).astype(bf16)


def call(kernel, name, outs, smem, *args):
    specs = [pl.BlockSpec(memory_space=pltpu.SMEM if i in smem else pltpu.VMEM) for i in range(len(args))]
    return pl.pallas_call(
        kernel,
        name=name,
        out_shape=[jax.ShapeDtypeStruct(s, d) for s, d in outs],
        in_specs=specs,
        out_specs=[pl.BlockSpec(memory_space=pltpu.VMEM) for _ in outs],
    )(*args)


def build(seq, head):
    def route(a, target):
        pairs = []
        for s in range(seq):
            for h in range(head):
                s2, h2 = target(s, h)
                if 0 <= s2 < seq:
                    pairs.append((s * head + h, s2 * head + h2))
        return lax.ppermute(a, ("seq", "head"), pairs)

    def partner(a):
        return route(a, lambda s, h: (s ^ 1, h))

    def chips(a, hops):
        return route(a, lambda s, h: (s + 2 * hops if s % 2 == 0 else s - 2 * hops, h))

    def head_sum(a):
        a = a + route(a, lambda s, h: (s, h ^ 1 if s % 2 == 0 else h ^ 3))
        return a + route(a, lambda s, h: (s, h ^ 3 if s % 2 == 0 else h ^ 1))

    def body(x, b, c, dt, rates, skips, docs, g):
        length, width = x.shape
        heads = dt.shape[0]
        place = lax.axis_index("seq").astype(jnp.int32).reshape(1)
        state = (STATE + 8, width)
        wide = (length, width)
        send, keep, xh, xl, gh, gl, facts, segs, segr, last = call(
            edge_kernel, "edges",
            [(state, f32), (state, f32), (wide, bf16), (wide, bf16), (wide, bf16), (wide, bf16),
             ((length, 2 * heads), f32), ((length, 8), f32), ((8, length), f32), ((8, width), f32)],
            (0, 1), place, rates, docs.reshape(1, -1), dt, x, g, b, c)
        got = partner(send)
        row = lax.broadcasted_iota(jnp.int32, state, 0)
        chip = jnp.where(row < STATE, got, 0.0) + got[STATE : STATE + 1] * keep
        near = chips(chip, 1)
        far = chips(chip, 2)
        y0, z0, grads = call(
            local_kernel, "local", [(wide, f32), (wide, f32), ((2 * length, STATE), f32)],
            (0,), skips, facts, segs, segr, x, g, xh, xl, gh, gl, b, c)
        mine = near[:STATE] + near[STATE : STATE + 1] * far[:STATE]
        other = partner(keep[:STATE] + keep[STATE : STATE + 1] * mine)
        (part,) = call(
            grad_kernel, "grads", [((2 * length, STATE), f32)],
            (0,), place, mine, other, last, segs, xh, xl, gh, gl, grads)
        y, z = call(
            out_kernel, "outs", [(wide, bf16), (wide, bf16)],
            (0,), place, mine, other, last, facts, segs, b, c, y0, z0)
        summed = head_sum(part)
        return y, z, summed[:length], summed[length:]

    return body


def solution(mesh):
    wide = P("seq", "head")
    row = P("seq", None)
    return jax.shard_map(
        build(mesh.shape["seq"], mesh.shape["head"]),
        mesh=mesh,
        in_specs=(wide, row, row, P("head", "seq"), P("head"), P("head"), P(), wide),
        out_specs=(wide, wide, row, row),
        check_vma=False,
    )
```

time: 420 us -> 54.1 us (0.13); the launches traced: 415 us -> 53.8 us
  blocking collectives: 112 us -> 0 us
  waiting for transfers between devices: 129 us -> 19.8 us
  other arithmetic: 74.1 us -> 3 us
  local copies, waits for them, and re-layouts: 53.9 us -> 1.48 us
  matrix products: 28.2 us -> 0 us
  Pallas kernels: 0 us -> 14.9 us
  between operations: 15.4 us -> 0.71 us
  starting transfers between devices: 0.12 us -> 13.9 us
    psum x1 -> x0, waiting for transfers between devices: 124 us -> none  [body(): grad_b, grad_c = lax.psum((grad_b, grad_c), 'head')]
    unnamed x1 -> x0, blocking collectives: 112 us -> none
    add x64 -> x4, other arithmetic: 68.7 us -> 3 us  [the longest x1 1.15 us: body(): chip = jnp.where(row < STATE, got, 0.0) + got[STATE:STATE + 1] * keep]
    mul x63 -> x0, local copies, waits for them, and re-layouts: 43.9 us -> none  [combine_pair(): later_part[0][:, None, None] * earlier[1] + later_part[1]]
    dot_general x16 -> x0, matrix products: 28.2 us -> none  [the longest x1 4.28 us: forward(): result = jnp.einsum('hts,shp->thp', mixing, scaled, precision=highest)]
    ppermute x0 -> x6, waiting for transfers between devices: none -> 19.8 us  [route(): return lax.ppermute(a, ('seq', 'head'), pairs)]
    pallas_call x0 -> x4, Pallas kernels: none -> 14.9 us  [call(): pl.pallas_call(kernel, name=name, out_shape=[jax.ShapeDtypeStruct(s, d) f...]
    ppermute x0 -> x6, starting transfers between devices: none -> 13.9 us  [route(): return lax.ppermute(a, ('seq', 'head'), pairs)]
  transfers between devices with their start and end apart: 3 -> 6, of which waited for: 2 -> 5; matrix products, arithmetic and copies ran while one was open for 26% -> 0% of each run, Pallas kernels for 0% -> 15%
where the time goes in v1:
time: 54.1 us; the launch traced here: 53.8 us
  waiting for transfers between devices  19.8 us (37%)
  Pallas kernels  14.9 us (28%)
  starting transfers between devices  13.9 us (26%)
  other arithmetic  3 us (6%)
  local copies, waits for them, and re-layouts  1.48 us (3%)
  between operations  0.71 us (1%)
    ppermute x6, waiting for transfers between devices, route(): return lax.ppermute(a, ('seq', 'head'), pairs)  19.8 us
    pallas_call x4, Pallas kernels, call(): pl.pallas_call(kernel, name=name, out_shape=[jax.ShapeDtypeStruct(s, d) f...  14.9 us
    ppermute x6, starting transfers between devices, route(): return lax.ppermute(a, ('seq', 'head'), pairs)  13.9 us
    add x1, other arithmetic, body(): chip = jnp.where(row < STATE, got, 0.0) + got[STATE:STATE + 1] * keep  1.15 us
  transfers between devices with their start and end apart: 6, of which 5 were waited for; matrix products, arithmetic and copies ran while one was open for 0% of the time, Pallas kernels for 15%

profile of v1, /device:TPU:6, one launch (start us, length us, event | category | flops | bytes accessed | tf_op | source)
XLA Modules:
  0.0 53.8 jit_solution(16525659696117264987)
XLA Ops:
  0.6 3.6 %edges.1 = (f32[136,640]{1,0:T(8,128)}, f32[136,640]{1,0:T(8,128)}, bf16[256,640]{1,0:T(8,128)(2,1)}, bf16[256,640]{1,0:T(8,128)(2,1)}, bf16[256,640]{1,0:T(8,12...) custom-call(s32[1]{0:T(128)} %bitcast.place, ...), custom_call_target="tpu_custom_call" | custom-call | tf_op jit(solution)/shard_map/edges/pallas_call | solution.py:168
  4.2 0.1 collective-permute-start
  4.3 1.8 %collective-permute-done = f32[136,640]{1,0:T(8,128)S(1)} collective-permute-done((f32[136,640]{1,0:T(8,128)}, f32[136,640]{1,0:T(8,128)S(1)}, u32[]{:S(2)}, u32[]{:S(2)}) %collective-permute-start) | collective-permute-done | bytes 348192 | tf_op jit(solution)/shard_map/ppermute | solution.py:185
  6.2 0.0 copy-start
  6.2 1.1 %multiply_add_fusion = f32[136,640]{1,0:T(8,128)S(1)} fusion(f32[136,640]{1,0:T(8,128)} %get-tuple-element.20, f32[136,640]{1,0:T(8,128)S(1)} %collective-permute-done, f32[640]{0:T(1024)S(1)} %slice_reduce_fusion.1, pred[136]{0:T(512)(128)(4,1)S(1)} %iota_compare_fusion), kind=kLoop, calls=%fused_computation | loop fusion | flops 261120 | bytes 1047176 | tf_op jit(solution)/shard_map/add | solution.py:210
  7.4 3.8 %collective-permute-start.1 = (f32[136,640]{1,0:T(8,128)S(1)}, f32[136,640]{1,0:T(8,128)S(1)}, u32[]{:S(2)}, u32[]{:S(2)}) collective-permute-start(f32[136,640]{1,0:T(8,128)S(1)} %multiply_add_fusion), channel_id=1, source_target_pairs={{0,8},{1,9},{2,10},{3,11},{8,16},{9,17},{10,18},{11,19},{12,4},{13... | collective-permute-start | bytes 1044488 | tf_op jit(solution)/shard_map/ppermute | solution.py:185
  11.2 5.2 %collective-permute-start.2 = (f32[136,640]{1,0:T(8,128)S(1)}, f32[136,640]{1,0:T(8,128)S(1)}, u32[]{:S(2)}, u32[]{:S(2)}) collective-permute-start(f32[136,640]{1,0:T(8,128)S(1)} %multiply_add_fusion), channel_id=1, source_target_pairs={{0,16},{1,17},{2,18},{3,19},{8,24},{9,25},{10,26},{11,27},{16,32},... | collective-permute-start | bytes 1044488 | tf_op jit(solution)/shard_map/ppermute | solution.py:185
  16.4 0.0 copy-done
  16.4 4.2 %collective-permute-done.1 = f32[136,640]{1,0:T(8,128)S(1)} collective-permute-done((f32[136,640]{1,0:T(8,128)S(1)}, f32[136,640]{1,0:T(8,128)S(1)}, u32[]{:S(2)}, u32[]{:S(2)}) %collective-permute-start.1) | collective-permute-done | bytes 348192 | tf_op jit(solution)/shard_map/ppermute | solution.py:185
  20.7 7.6 %collective-permute-done.2 = f32[136,640]{1,0:T(8,128)S(1)} collective-permute-done((f32[136,640]{1,0:T(8,128)S(1)}, f32[136,640]{1,0:T(8,128)S(1)}, u32[]{:S(2)}, u32[]{:S(2)}) %collective-permute-start.2) | collective-permute-done | bytes 348192 | tf_op jit(solution)/shard_map/ppermute | solution.py:185
  28.2 0.8 %multiply_add_fusion.1 = (f32[128,640]{1,0:T(8,128)S(1)}, f32[128,640]{1,0:T(8,128)}) fusion(f32[136,640]{1,0:T(8,128)S(1)} %copy-done, f32[640]{0:T(1024)S(1)} %slice_reduce_fusion.2, f32[136,640]{1,0:T(8,128)S(1)} %collective-permute-done.2, f32[640]{0:T(1024)S(1)} %slice_reduce_fusion, f32[136,640]{1,0:T(8,128)S(1)} %collective-permute-done.1), kind=kLoop, calls=%fused_computation.3 | loop fusion | flops 327680 | bytes 1643520 | tf_op jit(solution)/shard_map/add | solution.py:217
  29.1 0.0 collective-permute-start.3
  29.1 5.0 %local.1 = (f32[256,640]{1,0:T(8,128)}, f32[256,640]{1,0:T(8,128)}, f32[512,128]{1,0:T(8,128)}) custom-call(f32[10]{0:T(128)} %skips.1, f32[256,20]{1,0:T(8,128)} %get-tuple-element.22.facts, f32[256,8]{1,0:T(8,128)} %get-tuple-element.23.segs, f32[8,256]{1,0:T(8,128)} %get-tuple-element.24.segr, f32[256,640]{1,0:T(8,128)} %x.3, f32[256,640]{1,0:T(8,128)} %g.3, ...), custom_call_target="tpu_custom_call" | custom-call | tf_op jit(solution)/shard_map/local/pallas_call | solution.py:168
  34.0 0.0 collective-permute-done.3.other
  34.0 0.0 copy-start.1
  34.0 0.7 %copy-done.1 = f32[128,640]{1,0:T(8,128)} copy-done((f32[128,640]{1,0:T(8,128)}, f32[128,640]{1,0:T(8,128)S(1)}, u32[]{:S(2)}) %copy-start.1) | copy-done | bytes 327704
  34.8 3.0 %grads.1 = f32[512,128]{1,0:T(8,128)} custom-call(s32[1]{0:T(128)} %bitcast.place, f32[128,640]{1,0:T(8,128)} %get-tuple-element.35.mine, f32[128,640]{1,0:T(8,128)} %copy-done.1, f32[8,640]{1,0:T(8,128)} %get-tuple-element.21.last, f32[256,8]{1,0:T(8,128)} %get-tuple-element.23.segs, bf16[256,640]{1,0:T(8,128)(2,1)} %get-tuple-element.25.xh, ...), custom_call_target="tpu_custom_call" | custom-call | tf_op jit(solution)/shard_map/grads/pallas_call | solution.py:168
  37.8 1.7 %collective-permute-start.4 = (f32[512,128]{1,0:T(8,128)}, f32[512,128]{1,0:T(8,128)S(1)}, u32[]{:S(2)}, u32[]{:S(2)}) collective-permute-start(f32[512,128]{1,0:T(8,128)} %grads.1), channel_id=1, source_target_pairs={{0,1},{1,0},{2,3},{3,2},{4,7},{5,6},{6,5},{7,4},{8,9},{9,8},{10,11... | collective-permute-start | bytes 786440 | tf_op jit(solution)/shard_map/ppermute | solution.py:185
  39.5 4.9 %collective-permute-done.4 = f32[512,128]{1,0:T(8,128)S(1)} collective-permute-done((f32[512,128]{1,0:T(8,128)}, f32[512,128]{1,0:T(8,128)S(1)}, u32[]{:S(2)}, u32[]{:S(2)}) %collective-permute-start.4) | collective-permute-done | bytes 262176 | tf_op jit(solution)/shard_map/ppermute | solution.py:185
  44.4 1.0 %add.18 = f32[512,128]{1,0:T(8,128)S(1)} add(f32[512,128]{1,0:T(8,128)} %grads.1, f32[512,128]{1,0:T(8,128)S(1)} %collective-permute-done.4) | non-fusion elementwise | flops 65536 | bytes 786432 | tf_op jit(solution)/shard_map/add | solution.py:194
  45.4 3.1 %collective-permute-start.5 = (f32[512,128]{1,0:T(8,128)S(1)}, f32[512,128]{1,0:T(8,128)S(1)}, u32[]{:S(2)}, u32[]{:S(2)}) collective-permute-start(f32[512,128]{1,0:T(8,128)S(1)} %add.18), channel_id=1, source_target_pairs={{0,3},{1,2},{2,1},{3,0},{4,5},{5,4},{6,7},{7,6},{8,11},{9,10},{10,... | collective-permute-start | bytes 786440 | tf_op jit(solution)/shard_map/ppermute | solution.py:185
  48.5 3.3 %outs.1 = (bf16[256,640]{1,0:T(8,128)(2,1)}, bf16[256,640]{1,0:T(8,128)(2,1)}) custom-call(s32[1]{0:T(128)} %bitcast.place, f32[128,640]{1,0:T(8,128)} %get-tuple-element.35.mine, f32[128,640]{1,0:T(8,128)} %copy-done.1, f32[8,640]{1,0:T(8,128)} %get-tuple-element.21.last, f32[256,20]{1,0:T(8,128)} %get-tuple-element.22.facts, ...), custom_call_target="tpu_custom_call" | custom-call | tf_op jit(solution)/shard_map/outs/pallas_call | solution.py:168
  51.8 1.2 %collective-permute-done.5 = f32[512,128]{1,0:T(8,128)S(1)} collective-permute-done((f32[512,128]{1,0:T(8,128)S(1)}, f32[512,128]{1,0:T(8,128)S(1)}, u32[]{:S(2)}, u32[]{:S(2)}) %collective-permute-start.5) | collective-permute-done | bytes 262176 | tf_op jit(solution)/shard_map/ppermute | solution.py:185
  53.1 0.7 %fusion.2 = (f32[256,128]{1,0:T(8,128)}, f32[256,128]{1,0:T(8,128)}) fusion(f32[512,128]{1,0:T(8,128)S(1)} %add.19), kind=kLoop, calls=%fused_computation.8 | loop fusion | bytes 524288 | tf_op jit(solution)/shard_map/slice | solution.py:225
  (5 shorter events, 0.1 us)
Async XLA Ops:
  4.2 2.0 %collective-permute-start = (f32[136,640]{1,0:T(8,128)}, f32[136,640]{1,0:T(8,128)S(1)}, u32[]{:S(2)}, u32[]{:S(2)}) collective-permute-start(f32[136,640]{1,0:T(8,128)} %get-tuple-element.19), channel_id=1, source_target_pairs={{0,4},{1,5},{2,6},{3,7},{4,0},{5,1},{6,2},{7,3},{8,12},{9,13},{10,... | collective-permute-start | bytes 1044488 | tf_op jit(solution)/shard_map/ppermute | solution.py:185
  6.2 10.2 %copy-start = (f32[136,640]{1,0:T(8,128)S(1)}, f32[136,640]{1,0:T(8,128)}, u32[]{:S(2)}) copy-start(f32[136,640]{1,0:T(8,128)} %get-tuple-element.20) | copy-start | bytes 1044484
  7.4 13.3 %collective-permute-start.1 = (f32[136,640]{1,0:T(8,128)S(1)}, f32[136,640]{1,0:T(8,128)S(1)}, u32[]{:S(2)}, u32[]{:S(2)}) collective-permute-start(f32[136,640]{1,0:T(8,128)S(1)} %multiply_add_fusion), channel_id=1, source_target_pairs={{0,8},{1,9},{2,10},{3,11},{8,16},{9,17},{10,18},{11,19},{12,4},{13... | collective-permute-start | bytes 1044488 | tf_op jit(solution)/shard_map/ppermute | solution.py:185
  11.2 17.1 %collective-permute-start.2 = (f32[136,640]{1,0:T(8,128)S(1)}, f32[136,640]{1,0:T(8,128)S(1)}, u32[]{:S(2)}, u32[]{:S(2)}) collective-permute-start(f32[136,640]{1,0:T(8,128)S(1)} %multiply_add_fusion), channel_id=1, source_target_pairs={{0,16},{1,17},{2,18},{3,19},{8,24},{9,25},{10,26},{11,27},{16,32},... | collective-permute-start | bytes 1044488 | tf_op jit(solution)/shard_map/ppermute | solution.py:185
  29.1 5.0 %collective-permute-start.3 = (f32[128,640]{1,0:T(8,128)S(1)}, f32[128,640]{1,0:T(8,128)S(1)}, u32[]{:S(2)}, u32[]{:S(2)}) collective-permute-start(f32[128,640]{1,0:T(8,128)S(1)} %get-tuple-element.34), channel_id=1, source_target_pairs={{0,4},{1,5},{2,6},{3,7},{4,0},{5,1},{6,2},{7,3},{8,12},{9,13},{10,... | collective-permute-start | bytes 983048 | tf_op jit(solution)/shard_map/ppermute | solution.py:185
  34.0 0.7 %copy-start.1 = (f32[128,640]{1,0:T(8,128)}, f32[128,640]{1,0:T(8,128)S(1)}, u32[]{:S(2)}) copy-start(f32[128,640]{1,0:T(8,128)S(1)} %collective-permute-done.3.other) | copy-start | bytes 983044
  37.8 6.6 %collective-permute-start.4 = (f32[512,128]{1,0:T(8,128)}, f32[512,128]{1,0:T(8,128)S(1)}, u32[]{:S(2)}, u32[]{:S(2)}) collective-permute-start(f32[512,128]{1,0:T(8,128)} %grads.1), channel_id=1, source_target_pairs={{0,1},{1,0},{2,3},{3,2},{4,7},{5,6},{6,5},{7,4},{8,9},{9,8},{10,11... | collective-permute-start | bytes 786440 | tf_op jit(solution)/shard_map/ppermute | solution.py:185
  45.4 7.7 %collective-permute-start.5 = (f32[512,128]{1,0:T(8,128)S(1)}, f32[512,128]{1,0:T(8,128)S(1)}, u32[]{:S(2)}, u32[]{:S(2)}) collective-permute-start(f32[512,128]{1,0:T(8,128)S(1)} %add.18), channel_id=1, source_target_pairs={{0,3},{1,2},{2,1},{3,0},{4,5},{5,4},{6,7},{7,6},{8,11},{9,10},{10,... | collective-permute-start | bytes 786440 | tf_op jit(solution)/shard_map/ppermute | solution.py:185

commit v2 on v1

--- a/solution.py
+++ b/solution.py
@@ -187,8 +187,8 @@
     def partner(a):
         return route(a, lambda s, h: (s ^ 1, h))
 
-    def chips(a, hops):
-        return route(a, lambda s, h: (s + 2 * hops if s % 2 == 0 else s - 2 * hops, h))
+    def chips(a):
+        return route(a, lambda s, h: (s + 2 if s % 2 == 0 else s - 2, h))
 
     def head_sum(a):
         a = a + route(a, lambda s, h: (s, h ^ 1 if s % 2 == 0 else h ^ 3))
@@ -206,14 +206,14 @@
              ((length, 2 * heads), f32), ((length, 8), f32), ((8, length), f32), ((8, width), f32)],
             (0, 1), place, rates, docs.reshape(1, -1), dt, x, g, b, c)
         got = partner(send)
-        row = lax.broadcasted_iota(jnp.int32, state, 0)
-        chip = jnp.where(row < STATE, got, 0.0) + got[STATE : STATE + 1] * keep
-        near = chips(chip, 1)
-        far = chips(chip, 2)
+        state_out = got[:STATE] + got[STATE : STATE + 1] * keep[:STATE]
+        fade = got[STATE : STATE + 1] * keep[STATE : STATE + 1]
+        near = chips(state_out)
         y0, z0, grads = call(
             local_kernel, "local", [(wide, f32), (wide, f32), ((2 * length, STATE), f32)],
             (0,), skips, facts, segs, segr, x, g, xh, xl, gh, gl, b, c)
-        mine = near[:STATE] + near[STATE : STATE + 1] * far[:STATE]
+        near, grads = lax.optimization_barrier((near, grads))
+        mine = chips(state_out + fade * near)
         other = partner(keep[:STATE] + keep[STATE : STATE + 1] * mine)
         (part,) = call(
             grad_kernel, "grads", [((2 * length, STATE), f32)],

time: 54.1 us -> 54.8 us (1.013)
  waiting for transfers between devices: 19.8 us -> 23.1 us
  starting transfers between devices: 13.9 us -> 10.7 us
  local copies, waits for them, and re-layouts: 1.48 us -> 2.13 us
    ppermute x6, waiting for transfers between devices: 19.8 us -> 23.1 us  [route(): return lax.ppermute(a, ('seq', 'head'), pairs)]
    ppermute x6, starting transfers between devices: 13.9 us -> 10.7 us  [route(): return lax.ppermute(a, ('seq', 'head'), pairs)]
    add x1, other arithmetic: 0.83 us -> 0.04 us  [body(): other = partner(keep[:STATE] + keep[STATE:STATE + 1] * mine)]
    slice x0 -> x1, other arithmetic: none -> 0.75 us  [body(): fade = got[STATE:STATE + 1] * keep[STATE:STATE + 1]]
    unnamed x4 -> x6, local copies, waits for them, and re-layouts: 0.72 us -> 1.41 us
    add x1 -> x2, other arithmetic: 1.15 us -> 1.05 us  [the longest x1 1.01 us: body(): state_out = got[:STATE] + got[STATE:STATE + 1] * keep[:STATE]]
  transfers between devices with their start and end apart: 6 -> 6, of which waited for: 5 -> 6; matrix products, arithmetic and copies ran while one was open for 0% -> 0% of each run, Pallas kernels for 15% -> 15%
where the time goes in v2:
time: 54.8 us; the launch traced here: 54.4 us
  waiting for transfers between devices  23.1 us (42%)
  Pallas kernels  14.9 us (27%)
  starting transfers between devices  10.7 us (20%)
  other arithmetic  2.86 us (5%)
  local copies, waits for them, and re-layouts  2.13 us (4%)
  between operations  0.69 us (1%)
    ppermute x6, waiting for transfers between devices, route(): return lax.ppermute(a, ('seq', 'head'), pairs)  23.1 us
    pallas_call x4, Pallas kernels, call(): pl.pallas_call(kernel, name=name, out_shape=[jax.ShapeDtypeStruct(s, d) f...  14.9 us
    ppermute x6, starting transfers between devices, route(): return lax.ppermute(a, ('seq', 'head'), pairs)  10.7 us
    unnamed x6, local copies, waits for them, and re-layouts  1.41 us
  transfers between devices with their start and end apart: 6, of which 6 were waited for; matrix products, arithmetic and copies ran while one was open for 0% of the time, Pallas kernels for 15%

profile of v2, /device:TPU:6, one launch (start us, length us, event | category | flops | bytes accessed | tf_op | source)
XLA Modules:
  0.0 54.4 jit_solution(16608285915834581932)
XLA Ops:
  0.6 3.6 %edges.1 = (f32[136,640]{1,0:T(8,128)}, f32[136,640]{1,0:T(8,128)}, bf16[256,640]{1,0:T(8,128)(2,1)}, bf16[256,640]{1,0:T(8,128)(2,1)}, bf16[256,640]{1,0:T(8,12...) custom-call(s32[1]{0:T(128)} %bitcast.place, ...), custom_call_target="tpu_custom_call" | custom-call | tf_op jit(solution)/shard_map/edges/pallas_call | solution.py:168
  4.2 0.1 collective-permute-start
  4.3 1.9 %collective-permute-done = f32[136,640]{1,0:T(8,128)S(1)} collective-permute-done((f32[136,640]{1,0:T(8,128)}, f32[136,640]{1,0:T(8,128)S(1)}, u32[]{:S(2)}, u32[]{:S(2)}) %collective-permute-start) | collective-permute-done | bytes 348192 | tf_op jit(solution)/shard_map/ppermute | solution.py:185
  6.2 0.8 %slice_reduce_fusion.1 = (f32[640]{0:T(1024)S(1)}, f32[640]{0:T(1024)S(1)}, f32[640]{0:T(1024)S(1)}) fusion(f32[136,640]{1,0:T(8,128)} %get-tuple-element.22, f32[136,640]{1,0:T(8,128)S(1)} %collective-permute-done), kind=kLoop, calls=%fused_computation.5 | loop fusion | flops 640 | bytes 12800 | tf_op jit(solution)/shard_map/slice | solution.py:210
  6.9 1.0 %slice_add_fusion = f32[128,640]{1,0:T(8,128)S(1)} fusion(f32[136,640]{1,0:T(8,128)S(1)} %collective-permute-done, f32[136,640]{1,0:T(8,128)} %get-tuple-element.22, f32[640]{0:T(1024)S(1)} %get-tuple-element.40), kind=kLoop, calls=%fused_computation | loop fusion | flops 163840 | bytes 985600 | tf_op jit(solution)/shard_map/add | solution.py:209
  8.0 3.8 %collective-permute-start.1 = (f32[128,640]{1,0:T(8,128)S(1)}, f32[128,640]{1,0:T(8,128)S(1)}, u32[]{:S(2)}, u32[]{:S(2)}) collective-permute-start(f32[128,640]{1,0:T(8,128)S(1)} %slice_add_fusion), channel_id=1, source_target_pairs={{0,8},{1,9},{2,10},{3,11},{8,16},{9,17},{10,18},{11,19},{12,4},{13... | collective-permute-start | bytes 983048 | tf_op jit(solution)/shard_map/ppermute | solution.py:185
  11.8 5.0 %local.1 = (f32[256,640]{1,0:T(8,128)}, f32[256,640]{1,0:T(8,128)}, f32[512,128]{1,0:T(8,128)}) custom-call(f32[10]{0:T(128)} %skips.1, f32[256,20]{1,0:T(8,128)} %get-tuple-element.23.facts, f32[256,8]{1,0:T(8,128)} %get-tuple-element.24.segs, f32[8,256]{1,0:T(8,128)} %get-tuple-element.25.segr, f32[256,640]{1,0:T(8,128)} %x.3, f32[256,640]{1,0:T(8,128)} %g.3, ...), custom_call_target="tpu_custom_call" | custom-call | tf_op jit(solution)/shard_map/local/pallas_call | solution.py:168
  16.8 4.3 %collective-permute-done.1 = f32[128,640]{1,0:T(8,128)S(1)} collective-permute-done((f32[128,640]{1,0:T(8,128)S(1)}, f32[128,640]{1,0:T(8,128)S(1)}, u32[]{:S(2)}, u32[]{:S(2)}) %collective-permute-start.1) | collective-permute-done | bytes 327712 | tf_op jit(solution)/shard_map/ppermute | solution.py:185
  21.0 0.0 copy-start.2
  21.1 2.1 %collective-permute-start.2 = (f32[128,640]{1,0:T(8,128)S(1)}, f32[128,640]{1,0:T(8,128)S(1)}, u32[]{:S(2)}, u32[]{:S(2)}) collective-permute-start(f32[128,640]{1,0:T(8,128)S(1)} %multiply_add_fusion.1), channel_id=1, source_target_pairs={{0,8},{1,9},{2,10},{3,11},{8,16},{9,17},{10,18},{11,19},{12,4},{13... | collective-permute-start | bytes 983048 | tf_op jit(solution)/shard_map/ppermute | solution.py:185
  23.1 9.1 %collective-permute-done.2.mine = f32[128,640]{1,0:T(8,128)S(1)} collective-permute-done((f32[128,640]{1,0:T(8,128)S(1)}, f32[128,640]{1,0:T(8,128)S(1)}, u32[]{:S(2)}, u32[]{:S(2)}) %collective-permute-start.2) | collective-permute-done | bytes 327712 | tf_op jit(solution)/shard_map/ppermute | solution.py:185
  32.3 0.0 copy-start
  32.3 0.0 copy-done.2
  32.3 0.7 %copy-done = f32[128,640]{1,0:T(8,128)} copy-done((f32[128,640]{1,0:T(8,128)}, f32[128,640]{1,0:T(8,128)S(1)}, u32[]{:S(2)}) %copy-start) | copy-done | bytes 327704
  33.0 0.0 collective-permute-start.3
  33.0 1.6 %collective-permute-done.3.other = f32[128,640]{1,0:T(8,128)S(1)} collective-permute-done((f32[128,640]{1,0:T(8,128)S(1)}, f32[128,640]{1,0:T(8,128)S(1)}, u32[]{:S(2)}, u32[]{:S(2)}) %collective-permute-start.3) | collective-permute-done | bytes 327712 | tf_op jit(solution)/shard_map/ppermute | solution.py:185
  34.6 0.0 copy-start.1
  34.6 0.7 %copy-done.1 = f32[128,640]{1,0:T(8,128)} copy-done((f32[128,640]{1,0:T(8,128)}, f32[128,640]{1,0:T(8,128)S(1)}, u32[]{:S(2)}) %copy-start.1) | copy-done | bytes 327704
  35.4 3.0 %grads.1 = f32[512,128]{1,0:T(8,128)} custom-call(s32[1]{0:T(128)} %bitcast.place, f32[128,640]{1,0:T(8,128)} %copy-done, f32[128,640]{1,0:T(8,128)} %copy-done.1, f32[8,640]{1,0:T(8,128)} %get-tuple-element.32.last, f32[256,8]{1,0:T(8,128)} %get-tuple-element.24.segs, bf16[256,640]{1,0:T(8,128)(2,1)} %get-tuple-element.26.xh, ...), custom_call_target="tpu_custom_call" | custom-call | tf_op jit(solution)/shard_map/grads/pallas_call | solution.py:168
  38.4 1.6 %collective-permute-start.4 = (f32[512,128]{1,0:T(8,128)}, f32[512,128]{1,0:T(8,128)S(1)}, u32[]{:S(2)}, u32[]{:S(2)}) collective-permute-start(f32[512,128]{1,0:T(8,128)} %grads.1), channel_id=1, source_target_pairs={{0,1},{1,0},{2,3},{3,2},{4,7},{5,6},{6,5},{7,4},{8,9},{9,8},{10,11... | collective-permute-start | bytes 786440 | tf_op jit(solution)/shard_map/ppermute | solution.py:185
  40.0 5.0 %collective-permute-done.4 = f32[512,128]{1,0:T(8,128)S(1)} collective-permute-done((f32[512,128]{1,0:T(8,128)}, f32[512,128]{1,0:T(8,128)S(1)}, u32[]{:S(2)}, u32[]{:S(2)}) %collective-permute-start.4) | collective-permute-done | bytes 262176 | tf_op jit(solution)/shard_map/ppermute | solution.py:185
  45.0 1.0 %add.18 = f32[512,128]{1,0:T(8,128)S(1)} add(f32[512,128]{1,0:T(8,128)} %grads.1, f32[512,128]{1,0:T(8,128)S(1)} %collective-permute-done.4) | non-fusion elementwise | flops 65536 | bytes 786432 | tf_op jit(solution)/shard_map/add | solution.py:194
  46.0 3.1 %collective-permute-start.5 = (f32[512,128]{1,0:T(8,128)S(1)}, f32[512,128]{1,0:T(8,128)S(1)}, u32[]{:S(2)}, u32[]{:S(2)}) collective-permute-start(f32[512,128]{1,0:T(8,128)S(1)} %add.18), channel_id=1, source_target_pairs={{0,3},{1,2},{2,1},{3,0},{4,5},{5,4},{6,7},{7,6},{8,11},{9,10},{10,... | collective-permute-start | bytes 786440 | tf_op jit(solution)/shard_map/ppermute | solution.py:185
  49.1 3.3 %outs.1 = (bf16[256,640]{1,0:T(8,128)(2,1)}, bf16[256,640]{1,0:T(8,128)(2,1)}) custom-call(s32[1]{0:T(128)} %bitcast.place, f32[128,640]{1,0:T(8,128)} %copy-done, f32[128,640]{1,0:T(8,128)} %copy-done.1, f32[8,640]{1,0:T(8,128)} %get-tuple-element.32.last, f32[256,20]{1,0:T(8,128)} %get-tuple-element.23.facts, f32[256,8]{1,0:T(8,128)} %get-tuple-element.24.segs, ...), custom_call_target="tpu_custom_call" | custom-call | tf_op jit(solution)/shard_map/outs/pallas_call | solution.py:168
  52.4 1.2 %collective-permute-done.5 = f32[512,128]{1,0:T(8,128)S(1)} collective-permute-done((f32[512,128]{1,0:T(8,128)S(1)}, f32[512,128]{1,0:T(8,128)S(1)}, u32[]{:S(2)}, u32[]{:S(2)}) %collective-permute-start.5) | collective-permute-done | bytes 262176 | tf_op jit(solution)/shard_map/ppermute | solution.py:185
  53.7 0.7 %fusion = (f32[256,128]{1,0:T(8,128)}, f32[256,128]{1,0:T(8,128)}) fusion(f32[512,128]{1,0:T(8,128)S(1)} %add.19), kind=kLoop, calls=%fused_computation.6 | loop fusion | bytes 524288 | tf_op jit(solution)/shard_map/slice | solution.py:225
  (3 shorter events, 0.1 us)
Async XLA Ops:
  4.2 2.0 %collective-permute-start = (f32[136,640]{1,0:T(8,128)}, f32[136,640]{1,0:T(8,128)S(1)}, u32[]{:S(2)}, u32[]{:S(2)}) collective-permute-start(f32[136,640]{1,0:T(8,128)} %get-tuple-element.21), channel_id=1, source_target_pairs={{0,4},{1,5},{2,6},{3,7},{4,0},{5,1},{6,2},{7,3},{8,12},{9,13},{10,... | collective-permute-start | bytes 1044488 | tf_op jit(solution)/shard_map/ppermute | solution.py:185
  8.0 13.1 %collective-permute-start.1 = (f32[128,640]{1,0:T(8,128)S(1)}, f32[128,640]{1,0:T(8,128)S(1)}, u32[]{:S(2)}, u32[]{:S(2)}) collective-permute-start(f32[128,640]{1,0:T(8,128)S(1)} %slice_add_fusion), channel_id=1, source_target_pairs={{0,8},{1,9},{2,10},{3,11},{8,16},{9,17},{10,18},{11,19},{12,4},{13... | collective-permute-start | bytes 983048 | tf_op jit(solution)/shard_map/ppermute | solution.py:185
  21.0 11.3 %copy-start.2 = (f32[136,640]{1,0:T(8,128)S(1)}, f32[136,640]{1,0:T(8,128)}, u32[]{:S(2)}) copy-start(f32[136,640]{1,0:T(8,128)} %get-tuple-element.22) | copy-start | bytes 1044484
  21.1 11.2 %collective-permute-start.2 = (f32[128,640]{1,0:T(8,128)S(1)}, f32[128,640]{1,0:T(8,128)S(1)}, u32[]{:S(2)}, u32[]{:S(2)}) collective-permute-start(f32[128,640]{1,0:T(8,128)S(1)} %multiply_add_fusion.1), channel_id=1, source_target_pairs={{0,8},{1,9},{2,10},{3,11},{8,16},{9,17},{10,18},{11,19},{12,4},{13... | collective-permute-start | bytes 983048 | tf_op jit(solution)/shard_map/ppermute | solution.py:185
  32.3 0.7 %copy-start = (f32[128,640]{1,0:T(8,128)}, f32[128,640]{1,0:T(8,128)S(1)}, u32[]{:S(2)}) copy-start(f32[128,640]{1,0:T(8,128)S(1)} %collective-permute-done.2.mine) | copy-start | bytes 983044
  33.0 1.6 %collective-permute-start.3 = (f32[128,640]{1,0:T(8,128)S(1)}, f32[128,640]{1,0:T(8,128)S(1)}, u32[]{:S(2)}, u32[]{:S(2)}) collective-permute-start(f32[128,640]{1,0:T(8,128)S(1)} %multiply_add_fusion), channel_id=1, source_target_pairs={{0,4},{1,5},{2,6},{3,7},{4,0},{5,1},{6,2},{7,3},{8,12},{9,13},{10,... | collective-permute-start | bytes 983048 | tf_op jit(solution)/shard_map/ppermute | solution.py:185
  34.6 0.7 %copy-start.1 = (f32[128,640]{1,0:T(8,128)}, f32[128,640]{1,0:T(8,128)S(1)}, u32[]{:S(2)}) copy-start(f32[128,640]{1,0:T(8,128)S(1)} %collective-permute-done.3.other) | copy-start | bytes 983044
  38.4 6.6 %collective-permute-start.4 = (f32[512,128]{1,0:T(8,128)}, f32[512,128]{1,0:T(8,128)S(1)}, u32[]{:S(2)}, u32[]{:S(2)}) collective-permute-start(f32[512,128]{1,0:T(8,128)} %grads.1), channel_id=1, source_target_pairs={{0,1},{1,0},{2,3},{3,2},{4,7},{5,6},{6,5},{7,4},{8,9},{9,8},{10,11... | collective-permute-start | bytes 786440 | tf_op jit(solution)/shard_map/ppermute | solution.py:185
  46.0 7.7 %collective-permute-start.5 = (f32[512,128]{1,0:T(8,128)S(1)}, f32[512,128]{1,0:T(8,128)S(1)}, u32[]{:S(2)}, u32[]{:S(2)}) collective-permute-start(f32[512,128]{1,0:T(8,128)S(1)} %add.18), channel_id=1, source_target_pairs={{0,3},{1,2},{2,1},{3,0},{4,5},{5,4},{6,7},{7,6},{8,11},{9,10},{10,... | collective-permute-start | bytes 786440 | tf_op jit(solution)/shard_map/ppermute | solution.py:185

commit v3 on v2

--- a/solution.py
+++ b/solution.py
@@ -1,3 +1,5 @@
+from functools import partial
+
 import jax
 import jax.numpy as jnp
 from jax import lax
@@ -66,7 +68,7 @@
     return out
 
 
-def edge_kernel(place, rates, docs, dt, x, g, b, c, send, keep, xh, xl, gh, gl, facts, segs, segr, last):
+def edge_kernel(place, rates, docs, dt, x, g, b, c, send, keep, mh, ml, oh, ol, facts, segs, segr, last):
     length, width = x.shape
     heads = dt.shape[0]
     core = place[0] % 2
@@ -101,22 +103,31 @@
     total = grow_x[length - 1 :, :]
     x_parts = halves(x[...] * shrink_x)
     g_parts = halves(g[...] * grow_x)
-    xh[...], xl[...] = x_parts
-    gh[...], gl[...] = g_parts
+    is_zero = core == 0
+
+    @pl.when(is_zero)
+    def _():
+        mh[...], ml[...] = g_parts
+        oh[...], ol[...] = x_parts
+
+    @pl.when(core == 1)
+    def _():
+        mh[...], ml[...] = x_parts
+        oh[...], ol[...] = g_parts
+
     b_parts = halves((b[...] * final).T)
     c_parts = halves((c[...] * entry).T)
     end = dot3(b_parts, x_parts, NN) * total
     start = dot3(c_parts, g_parts, NN)
     last[...] = jnp.broadcast_to(total, (8, width))
     whole = jnp.broadcast_to(total * through, (8, width))
-    is_zero = core == 0
     send[:STATE, :] = jnp.where(is_zero, start, end)
     keep[:STATE, :] = jnp.where(is_zero, end, start)
     send[STATE:, :] = whole
     keep[STATE:, :] = whole
 
 
-def local_kernel(skips, facts, segs, segr, x, g, xh, xl, gh, gl, b, c, y0, z0, grads):
+def local_kernel(place, skips, facts, segs, segr, x, g, mh, ml, oh, ol, b, c, y0, z0, mine, other):
     length, width = x.shape
     heads = facts.shape[1] // 2
     b_parts = halves(b[...])
@@ -126,28 +137,28 @@
     same = segs[:, :1] == segr[:1, :]
     mask = jnp.where(same & (s_at <= t_at), 1.0, 0.0)
     mask_t = jnp.where(same & (t_at <= s_at), 1.0, 0.0)
-    x_parts = (xh[...], xl[...])
-    g_parts = (gh[...], gl[...])
+    core = place[0] % 2
+    m_parts = (mh[...], ml[...])
+    o_parts = (oh[...], ol[...])
+    x_parts = [jnp.where(core == 0, o, m) for m, o in zip(m_parts, o_parts)]
+    g_parts = [jnp.where(core == 0, m, o) for m, o in zip(m_parts, o_parts)]
     mix = halves(dot3(c_parts, b_parts, NT) * mask)
     mix_t = halves(dot3(b_parts, c_parts, NT) * mask_t)
     skip = head_row(skips, heads, width)
     y0[...] = dot3(mix, x_parts, NN) * spread(facts[:, :heads], heads, width) + skip * x[...]
     z0[...] = dot3(mix_t, g_parts, NN) * spread(facts[:, heads:], heads, width) + skip * g[...]
     weight = dot3(g_parts, x_parts, NT) * mask
-    grads[:length, :] = dot3(halves(weight.T), c_parts, NN)
-    grads[length:, :] = dot3(halves(weight), b_parts, NN)
-
-
-def grad_kernel(place, mine, other, last, segs, xh, xl, gh, gl, grads, total):
-    length, width = xh.shape
-    is_zero = place[0] % 2 == 0
-    mine_, other_ = mine[...], other[...]
-    into = jnp.where(is_zero, mine_, other_)
-    after = jnp.where(is_zero, other_, mine_) * last[:1, :]
-    grad_b = dot3((xh[...], xl[...]), halves(after), NT) * segs[:, 2:3]
-    grad_c = dot3((gh[...], gl[...]), halves(into), NT) * segs[:, 1:2]
-    total[:length, :] = grads[:length, :] + grad_b
-    total[length:, :] = grads[length:, :] + grad_c
+    grad_b = dot3(halves(weight.T), c_parts, NN)
+    grad_c = dot3(halves(weight), b_parts, NN)
+    mine[...] = jnp.where(core == 0, grad_c, grad_b)
+    other[...] = jnp.where(core == 0, grad_b, grad_c)
+
+
+def grad_kernel(core, place, state, last, segs, high, low, local, total):
+    is_forward = place[0] % 2 == core
+    scale = jnp.where(is_forward, 1.0, last[:1, :])
+    tokens = jnp.where(is_forward, segs[:, 1:2], segs[:, 2:3])
+    total[...] = local[...] + dot3((high[...], low[...]), halves(state[...] * scale), NT) * tokens
 
 
 def out_kernel(place, mine, other, last, facts, segs, b, c, y0, z0, y, z):
@@ -200,7 +211,7 @@
         place = lax.axis_index("seq").astype(jnp.int32).reshape(1)
         state = (STATE + 8, width)
         wide = (length, width)
-        send, keep, xh, xl, gh, gl, facts, segs, segr, last = call(
+        send, keep, mh, ml, oh, ol, facts, segs, segr, last = call(
             edge_kernel, "edges",
             [(state, f32), (state, f32), (wide, bf16), (wide, bf16), (wide, bf16), (wide, bf16),
              ((length, 2 * heads), f32), ((length, 8), f32), ((8, length), f32), ((8, width), f32)],
@@ -209,20 +220,22 @@
         state_out = got[:STATE] + got[STATE : STATE + 1] * keep[:STATE]
         fade = got[STATE : STATE + 1] * keep[STATE : STATE + 1]
         near = chips(state_out)
-        y0, z0, grads = call(
-            local_kernel, "local", [(wide, f32), (wide, f32), ((2 * length, STATE), f32)],
-            (0,), skips, facts, segs, segr, x, g, xh, xl, gh, gl, b, c)
-        near, grads = lax.optimization_barrier((near, grads))
+        thin = ((length, STATE), f32)
+        y0, z0, mine0, other0 = call(
+            local_kernel, "local", [(wide, f32), (wide, f32), thin, thin],
+            (0, 1), place, skips, facts, segs, segr, x, g, mh, ml, oh, ol, b, c)
+        near, mine0 = lax.optimization_barrier((near, mine0))
         mine = chips(state_out + fade * near)
         other = partner(keep[:STATE] + keep[STATE : STATE + 1] * mine)
-        (part,) = call(
-            grad_kernel, "grads", [((2 * length, STATE), f32)],
-            (0,), place, mine, other, last, segs, xh, xl, gh, gl, grads)
+        (first,) = call(partial(grad_kernel, 0), "first", [thin], (0,), place, mine, last, segs, mh, ml, mine0)
+        (second,) = call(partial(grad_kernel, 1), "second", [thin], (0,), place, other, last, segs, oh, ol, other0)
         y, z = call(
             out_kernel, "outs", [(wide, bf16), (wide, bf16)],
             (0,), place, mine, other, last, facts, segs, b, c, y0, z0)
-        summed = head_sum(part)
-        return y, z, summed[:length], summed[length:]
+        first = head_sum(first)
+        second = head_sum(second)
+        zero = (place[0] & 1) == 0
+        return y, z, jnp.where(zero, second, first), jnp.where(zero, first, second)
 
     return body
 

time: 54.8 us -> 53.8 us (0.982)
  waiting for transfers between devices: 23.1 us -> 19.2 us
  Pallas kernels: 14.9 us -> 16.9 us
  starting transfers between devices: 10.7 us -> 12.6 us
  local copies, waits for them, and re-layouts: 2.13 us -> 1.41 us
    ppermute x6 -> x8, waiting for transfers between devices: 23.1 us -> 19.2 us  [route(): return lax.ppermute(a, ('seq', 'head'), pairs)]
    pallas_call x4 -> x5, Pallas kernels: 14.9 us -> 16.9 us  [call(): pl.pallas_call(kernel, name=name, out_shape=[jax.ShapeDtypeStruct(s, d) f...]
    ppermute x6 -> x8, starting transfers between devices: 10.7 us -> 12.6 us  [route(): return lax.ppermute(a, ('seq', 'head'), pairs)]
    add x1 -> x2, other arithmetic: 0.99 us -> 0.03 us  [head_sum(): a = a + route(a, lambda s, h: (s, h ^ 1 if s % 2 == 0 else h ^ 3))]
    select_n x0 -> x1, other arithmetic: none -> 0.73 us  [body(): jnp.where(zero, first, second)]
    slice x1 -> x0, local copies, waits for them, and re-layouts: 0.72 us -> none  [body(): return (y, z, summed[:length], summed[length:])]
    unnamed x6 -> x10, local copies, waits for them, and re-layouts: 1.41 us -> 1.41 us
  transfers between devices with their start and end apart: 6 -> 8, of which waited for: 6 -> 5; matrix products, arithmetic and copies ran while one was open for 0% -> 0% of each run, Pallas kernels for 15% -> 24%
where the time goes in v3:
time: 53.8 us; the launch traced here: 53.4 us
  waiting for transfers between devices  19.2 us (36%)
  Pallas kernels  16.9 us (31%)
  starting transfers between devices  12.6 us (23%)
  other arithmetic  2.61 us (5%)
  local copies, waits for them, and re-layouts  1.41 us (3%)
  between operations  0.7 us (1%)
    ppermute x8, waiting for transfers between devices, route(): return lax.ppermute(a, ('seq', 'head'), pairs)  19.2 us
    pallas_call x5, Pallas kernels, call(): pl.pallas_call(kernel, name=name, out_shape=[jax.ShapeDtypeStruct(s, d) f...  16.9 us
    ppermute x8, starting transfers between devices, route(): return lax.ppermute(a, ('seq', 'head'), pairs)  12.6 us
    unnamed x10, local copies, waits for them, and re-layouts  1.41 us
  transfers between devices with their start and end apart: 8, of which 5 were waited for; matrix products, arithmetic and copies ran while one was open for 0% of the time, Pallas kernels for 24%

profile of v3, /device:TPU:6, one launch (start us, length us, event | category | flops | bytes accessed | tf_op | source)
XLA Modules:
  0.0 53.4 jit_solution(660878590308528458)
XLA Ops:
  0.6 3.8 %edges.1 = (f32[136,640]{1,0:T(8,128)}, f32[136,640]{1,0:T(8,128)}, bf16[256,640]{1,0:T(8,128)(2,1)}, bf16[256,640]{1,0:T(8,128)(2,1)}, bf16[256,640]{1,0:T(8,12...) custom-call(s32[1]{0:T(128)} %bitcast.place, ...), custom_call_target="tpu_custom_call" | custom-call | tf_op jit(solution)/shard_map/edges/pallas_call | solution.py:179
  4.5 0.1 collective-permute-start
  4.6 1.9 %collective-permute-done = f32[136,640]{1,0:T(8,128)S(1)} collective-permute-done((f32[136,640]{1,0:T(8,128)}, f32[136,640]{1,0:T(8,128)S(1)}, u32[]{:S(2)}, u32[]{:S(2)}) %collective-permute-start) | collective-permute-done | bytes 348192 | tf_op jit(solution)/shard_map/ppermute | solution.py:196
  6.4 0.8 %slice_reduce_fusion.1 = (f32[640]{0:T(1024)S(1)}, f32[640]{0:T(1024)S(1)}, f32[640]{0:T(1024)S(1)}) fusion(f32[136,640]{1,0:T(8,128)} %get-tuple-element.23, f32[136,640]{1,0:T(8,128)S(1)} %collective-permute-done), kind=kLoop, calls=%fused_computation.7 | loop fusion | flops 640 | bytes 12800 | tf_op jit(solution)/shard_map/slice | solution.py:221
  7.2 1.0 %slice_add_fusion = f32[128,640]{1,0:T(8,128)S(1)} fusion(f32[136,640]{1,0:T(8,128)S(1)} %collective-permute-done, f32[136,640]{1,0:T(8,128)} %get-tuple-element.23, f32[640]{0:T(1024)S(1)} %get-tuple-element.42), kind=kLoop, calls=%fused_computation | loop fusion | flops 163840 | bytes 985600 | tf_op jit(solution)/shard_map/add | solution.py:220
  8.2 3.8 %collective-permute-start.1 = (f32[128,640]{1,0:T(8,128)S(1)}, f32[128,640]{1,0:T(8,128)S(1)}, u32[]{:S(2)}, u32[]{:S(2)}) collective-permute-start(f32[128,640]{1,0:T(8,128)S(1)} %slice_add_fusion), channel_id=1, source_target_pairs={{0,8},{1,9},{2,10},{3,11},{8,16},{9,17},{10,18},{11,19},{12,4},{13... | collective-permute-start | bytes 983048 | tf_op jit(solution)/shard_map/ppermute | solution.py:196
  12.0 5.0 %local.1 = (f32[256,640]{1,0:T(8,128)}, f32[256,640]{1,0:T(8,128)}, f32[256,128]{1,0:T(8,128)}, f32[256,128]{1,0:T(8,128)}) custom-call(s32[1]{0:T(128)} %bitcast.place, f32[10]{0:T(128)} %skips.1, f32[256,20]{1,0:T(8,128)} %get-tuple-element.24.facts, f32[256,8]{1,0:T(8,128)} %get-tuple-element.25.segs, f32[8,256]{1,0:T(8,128)} %get-tuple-element.26.segr, ...), custom_call_target="tpu_custom_call" | custom-call | tf_op jit(solution)/shard_map/local/pallas_call | solution.py:179
  17.0 4.2 %collective-permute-done.1 = f32[128,640]{1,0:T(8,128)S(1)} collective-permute-done((f32[128,640]{1,0:T(8,128)S(1)}, f32[128,640]{1,0:T(8,128)S(1)}, u32[]{:S(2)}, u32[]{:S(2)}) %collective-permute-start.1) | collective-permute-done | bytes 327712 | tf_op jit(solution)/shard_map/ppermute | solution.py:196
  21.3 0.0 copy-start.2
  21.3 2.1 %collective-permute-start.2 = (f32[128,640]{1,0:T(8,128)S(1)}, f32[128,640]{1,0:T(8,128)S(1)}, u32[]{:S(2)}, u32[]{:S(2)}) collective-permute-start(f32[128,640]{1,0:T(8,128)S(1)} %multiply_add_fusion.1), channel_id=1, source_target_pairs={{0,8},{1,9},{2,10},{3,11},{8,16},{9,17},{10,18},{11,19},{12,4},{13... | collective-permute-start | bytes 983048 | tf_op jit(solution)/shard_map/ppermute | solution.py:196
  23.4 9.1 %collective-permute-done.2.mine.state = f32[128,640]{1,0:T(8,128)S(1)} collective-permute-done((f32[128,640]{1,0:T(8,128)S(1)}, f32[128,640]{1,0:T(8,128)S(1)}, u32[]{:S(2)}, u32[]{:S(2)}) %collective-permute-start.2) | collective-permute-done | bytes 327712 | tf_op jit(solution)/shard_map/ppermute | solution.py:196
  32.5 0.0 copy-start
  32.5 0.0 copy-done.2
  32.5 0.1 multiply_add_fusion
  32.6 0.7 %copy-done = f32[128,640]{1,0:T(8,128)} copy-done((f32[128,640]{1,0:T(8,128)}, f32[128,640]{1,0:T(8,128)S(1)}, u32[]{:S(2)}) %copy-start) | copy-done | bytes 327704
  33.3 0.0 collective-permute-start.3
  33.3 2.4 %first.1 = f32[256,128]{1,0:T(8,128)} custom-call(s32[1]{0:T(128)} %bitcast.place, f32[128,640]{1,0:T(8,128)} %copy-done, f32[8,640]{1,0:T(8,128)} %get-tuple-element.33.last, f32[256,8]{1,0:T(8,128)} %get-tuple-element.25.segs, bf16[256,640]{1,0:T(8,128)(2,1)} %get-tuple-element.27.mh.high, bf16[256,640]{1,0:T(8,128)(2,1)} %get-tuple-element.28.ml.low, ...), custom_call_target="tpu_custom_call" | custom-call | tf_op jit(solution)/shard_map/first/pallas_call | solution.py:179
  35.6 1.6 %collective-permute-start.6 = (f32[256,128]{1,0:T(8,128)}, f32[256,128]{1,0:T(8,128)S(1)}, u32[]{:S(2)}, u32[]{:S(2)}) collective-permute-start(f32[256,128]{1,0:T(8,128)} %first.1), channel_id=1, source_target_pairs={{0,1},{1,0},{2,3},{3,2},{4,7},{5,6},{6,5},{7,4},{8,9},{9,8},{10,11... | collective-permute-start | bytes 393224 | tf_op jit(solution)/shard_map/ppermute | solution.py:196
  37.2 0.0 collective-permute-done.3.other.state
  37.2 0.0 copy-start.1
  37.2 0.7 %copy-done.1 = f32[128,640]{1,0:T(8,128)} copy-done((f32[128,640]{1,0:T(8,128)}, f32[128,640]{1,0:T(8,128)S(1)}, u32[]{:S(2)}) %copy-start.1) | copy-done | bytes 327704
  37.9 0.0 copy-start.3
  37.9 2.4 %second.1 = f32[256,128]{1,0:T(8,128)} custom-call(s32[1]{0:T(128)} %bitcast.place, f32[128,640]{1,0:T(8,128)} %copy-done.1, f32[8,640]{1,0:T(8,128)} %get-tuple-element.33.last, f32[256,8]{1,0:T(8,128)} %get-tuple-element.25.segs, bf16[256,640]{1,0:T(8,128)(2,1)} %get-tuple-element.29.oh.high, bf16[256,640]{1,0:T(8,128)(2,1)} %get-tuple-element.30.ol.low, ...), custom_call_target="tpu_custom_call" | custom-call | tf_op jit(solution)/shard_map/second/pallas_call | solution.py:179
  40.3 0.0 copy-start.4
  40.3 0.5 collective-permute-start.4
  40.8 0.0 collective-permute-done.6
  40.8 0.0 copy-done.3
  40.8 3.1 %collective-permute-start.7 = (f32[256,128]{1,0:T(8,128)S(1)}, f32[256,128]{1,0:T(8,128)S(1)}, u32[]{:S(2)}, u32[]{:S(2)}) collective-permute-start(f32[256,128]{1,0:T(8,128)S(1)} %add.26), channel_id=1, source_target_pairs={{0,3},{1,2},{2,1},{3,0},{4,5},{5,4},{6,7},{7,6},{8,11},{9,10},{10,... | collective-permute-start | bytes 393224 | tf_op jit(solution)/shard_map/ppermute | solution.py:196
  43.9 2.4 %collective-permute-done.4 = f32[256,128]{1,0:T(8,128)S(1)} collective-permute-done((f32[256,128]{1,0:T(8,128)}, f32[256,128]{1,0:T(8,128)S(1)}, u32[]{:S(2)}, u32[]{:S(2)}) %collective-permute-start.4) | collective-permute-done | bytes 131104 | tf_op jit(solution)/shard_map/ppermute | solution.py:196
  46.3 0.0 copy-done.4
  46.4 1.4 %collective-permute-start.5 = (f32[256,128]{1,0:T(8,128)S(1)}, f32[256,128]{1,0:T(8,128)S(1)}, u32[]{:S(2)}, u32[]{:S(2)}) collective-permute-start(f32[256,128]{1,0:T(8,128)S(1)} %add.24), channel_id=1, source_target_pairs={{0,3},{1,2},{2,1},{3,0},{4,5},{5,4},{6,7},{7,6},{8,11},{9,10},{10,... | collective-permute-start | bytes 393224 | tf_op jit(solution)/shard_map/ppermute | solution.py:196
  47.8 3.3 %outs.1 = (bf16[256,640]{1,0:T(8,128)(2,1)}, bf16[256,640]{1,0:T(8,128)(2,1)}) custom-call(s32[1]{0:T(128)} %bitcast.place, f32[128,640]{1,0:T(8,128)} %copy-done, f32[128,640]{1,0:T(8,128)} %copy-done.1, f32[8,640]{1,0:T(8,128)} %get-tuple-element.33.last, f32[256,20]{1,0:T(8,128)} %get-tuple-element.24.facts, f32[256,8]{1,0:T(8,128)} %get-tuple-element.25.segs, ...), custom_call_target="tpu_custom_call" | custom-call | tf_op jit(solution)/shard_map/outs/pallas_call | solution.py:179
  51.1 0.0 collective-permute-done.7
  51.1 1.5 %collective-permute-done.5 = f32[256,128]{1,0:T(8,128)S(1)} collective-permute-done((f32[256,128]{1,0:T(8,128)S(1)}, f32[256,128]{1,0:T(8,128)S(1)}, u32[]{:S(2)}, u32[]{:S(2)}) %collective-permute-start.5) | collective-permute-done | bytes 131104 | tf_op jit(solution)/shard_map/ppermute | solution.py:196
  52.6 0.7 %broadcast_select_fusion = (f32[256,128]{1,0:T(8,128)}, f32[256,128]{1,0:T(8,128)}) fusion(pred[]{:T(512)S(6)} %eq.3, f32[256,128]{1,0:T(8,128)S(1)} %add.26, f32[256,128]{1,0:T(8,128)S(1)} %collective-permute-done.7, f32[256,128]{1,0:T(8,128)S(1)} %add.24, f32[256,128]{1,0:T(8,128)S(1)} %collective-permute-done.5), kind=kLoop, calls=%fused_computation.3 | loop fusion | flops 131072 | bytes 786433 | tf_op jit(solution)/shard_map/jit(_where)/select_n | solution.py:238
  (3 shorter events, 0.1 us)
Async XLA Ops:
  4.5 2.0 %collective-permute-start = (f32[136,640]{1,0:T(8,128)}, f32[136,640]{1,0:T(8,128)S(1)}, u32[]{:S(2)}, u32[]{:S(2)}) collective-permute-start(f32[136,640]{1,0:T(8,128)} %get-tuple-element.22), channel_id=1, source_target_pairs={{0,4},{1,5},{2,6},{3,7},{4,0},{5,1},{6,2},{7,3},{8,12},{9,13},{10,... | collective-permute-start | bytes 1044488 | tf_op jit(solution)/shard_map/ppermute | solution.py:196
  8.2 13.1 %collective-permute-start.1 = (f32[128,640]{1,0:T(8,128)S(1)}, f32[128,640]{1,0:T(8,128)S(1)}, u32[]{:S(2)}, u32[]{:S(2)}) collective-permute-start(f32[128,640]{1,0:T(8,128)S(1)} %slice_add_fusion), channel_id=1, source_target_pairs={{0,8},{1,9},{2,10},{3,11},{8,16},{9,17},{10,18},{11,19},{12,4},{13... | collective-permute-start | bytes 983048 | tf_op jit(solution)/shard_map/ppermute | solution.py:196
  21.3 11.3 %copy-start.2 = (f32[136,640]{1,0:T(8,128)S(1)}, f32[136,640]{1,0:T(8,128)}, u32[]{:S(2)}) copy-start(f32[136,640]{1,0:T(8,128)} %get-tuple-element.23) | copy-start | bytes 1044484
  21.3 11.2 %collective-permute-start.2 = (f32[128,640]{1,0:T(8,128)S(1)}, f32[128,640]{1,0:T(8,128)S(1)}, u32[]{:S(2)}, u32[]{:S(2)}) collective-permute-start(f32[128,640]{1,0:T(8,128)S(1)} %multiply_add_fusion.1), channel_id=1, source_target_pairs={{0,8},{1,9},{2,10},{3,11},{8,16},{9,17},{10,18},{11,19},{12,4},{13... | collective-permute-start | bytes 983048 | tf_op jit(solution)/shard_map/ppermute | solution.py:196
  32.5 0.7 %copy-start = (f32[128,640]{1,0:T(8,128)}, f32[128,640]{1,0:T(8,128)S(1)}, u32[]{:S(2)}) copy-start(f32[128,640]{1,0:T(8,128)S(1)} %collective-permute-done.2.mine.state) | copy-start | bytes 983044
  33.3 3.9 %collective-permute-start.3 = (f32[128,640]{1,0:T(8,128)S(1)}, f32[128,640]{1,0:T(8,128)S(1)}, u32[]{:S(2)}, u32[]{:S(2)}) collective-permute-start(f32[128,640]{1,0:T(8,128)S(1)} %multiply_add_fusion), channel_id=1, source_target_pairs={{0,4},{1,5},{2,6},{3,7},{4,0},{5,1},{6,2},{7,3},{8,12},{9,13},{10,... | collective-permute-start | bytes 983048 | tf_op jit(solution)/shard_map/ppermute | solution.py:196
  35.6 5.2 %collective-permute-start.6 = (f32[256,128]{1,0:T(8,128)}, f32[256,128]{1,0:T(8,128)S(1)}, u32[]{:S(2)}, u32[]{:S(2)}) collective-permute-start(f32[256,128]{1,0:T(8,128)} %first.1), channel_id=1, source_target_pairs={{0,1},{1,0},{2,3},{3,2},{4,7},{5,6},{6,5},{7,4},{8,9},{9,8},{10,11... | collective-permute-start | bytes 393224 | tf_op jit(solution)/shard_map/ppermute | solution.py:196
  37.2 0.7 %copy-start.1 = (f32[128,640]{1,0:T(8,128)}, f32[128,640]{1,0:T(8,128)S(1)}, u32[]{:S(2)}) copy-start(f32[128,640]{1,0:T(8,128)S(1)} %collective-permute-done.3.other.state) | copy-start | bytes 983044
  37.9 2.9 %copy-start.3 = (f32[256,128]{1,0:T(8,128)S(1)}, f32[256,128]{1,0:T(8,128)}, u32[]{:S(2)}) copy-start(f32[256,128]{1,0:T(8,128)} %first.1) | copy-start | bytes 393220
  40.3 6.0 %copy-start.4 = (f32[256,128]{1,0:T(8,128)S(1)}, f32[256,128]{1,0:T(8,128)}, u32[]{:S(2)}) copy-start(f32[256,128]{1,0:T(8,128)} %second.1) | copy-start | bytes 393220
  40.3 6.0 %collective-permute-start.4 = (f32[256,128]{1,0:T(8,128)}, f32[256,128]{1,0:T(8,128)S(1)}, u32[]{:S(2)}, u32[]{:S(2)}) collective-permute-start(f32[256,128]{1,0:T(8,128)} %second.1), channel_id=1, source_target_pairs={{0,1},{1,0},{2,3},{3,2},{4,7},{5,6},{6,5},{7,4},{8,9},{9,8},{10,11... | collective-permute-start | bytes 393224 | tf_op jit(solution)/shard_map/ppermute | solution.py:196
  40.8 10.3 %collective-permute-start.7 = (f32[256,128]{1,0:T(8,128)S(1)}, f32[256,128]{1,0:T(8,128)S(1)}, u32[]{:S(2)}, u32[]{:S(2)}) collective-permute-start(f32[256,128]{1,0:T(8,128)S(1)} %add.26), channel_id=1, source_target_pairs={{0,3},{1,2},{2,1},{3,0},{4,5},{5,4},{6,7},{7,6},{8,11},{9,10},{10,... | collective-permute-start | bytes 393224 | tf_op jit(solution)/shard_map/ppermute | solution.py:196
  46.4 6.3 %collective-permute-start.5 = (f32[256,128]{1,0:T(8,128)S(1)}, f32[256,128]{1,0:T(8,128)S(1)}, u32[]{:S(2)}, u32[]{:S(2)}) collective-permute-start(f32[256,128]{1,0:T(8,128)S(1)} %add.24), channel_id=1, source_target_pairs={{0,3},{1,2},{2,1},{3,0},{4,5},{5,4},{6,7},{7,6},{8,11},{9,10},{10,... | collective-permute-start | bytes 393224 | tf_op jit(solution)/shard_map/ppermute | solution.py:196

commit v4 on v3

--- a/solution.py
+++ b/solution.py
@@ -198,8 +198,8 @@
     def partner(a):
         return route(a, lambda s, h: (s ^ 1, h))
 
-    def chips(a):
-        return route(a, lambda s, h: (s + 2 if s % 2 == 0 else s - 2, h))
+    def chips(a, hops):
+        return route(a, lambda s, h: (s + 2 * hops if s % 2 == 0 else s - 2 * hops, h))
 
     def head_sum(a):
         a = a + route(a, lambda s, h: (s, h ^ 1 if s % 2 == 0 else h ^ 3))
@@ -217,15 +217,16 @@
              ((length, 2 * heads), f32), ((length, 8), f32), ((8, length), f32), ((8, width), f32)],
             (0, 1), place, rates, docs.reshape(1, -1), dt, x, g, b, c)
         got = partner(send)
-        state_out = got[:STATE] + got[STATE : STATE + 1] * keep[:STATE]
-        fade = got[STATE : STATE + 1] * keep[STATE : STATE + 1]
-        near = chips(state_out)
+        row = lax.broadcasted_iota(jnp.int32, state, 0)
+        chip = jnp.where(row < STATE, got, 0.0) + got[STATE : STATE + 1] * keep
+        far = chips(chip, 2)
+        near = chips(chip, 1)
         thin = ((length, STATE), f32)
         y0, z0, mine0, other0 = call(
             local_kernel, "local", [(wide, f32), (wide, f32), thin, thin],
             (0, 1), place, skips, facts, segs, segr, x, g, mh, ml, oh, ol, b, c)
-        near, mine0 = lax.optimization_barrier((near, mine0))
-        mine = chips(state_out + fade * near)
+        near, far, mine0 = lax.optimization_barrier((near, far, mine0))
+        mine = near[:STATE] + near[STATE : STATE + 1] * far[:STATE]
         other = partner(keep[:STATE] + keep[STATE : STATE + 1] * mine)
         (first,) = call(partial(grad_kernel, 0), "first", [thin], (0,), place, mine, last, segs, mh, ml, mine0)
         (second,) = call(partial(grad_kernel, 1), "second", [thin], (0,), place, other, last, segs, oh, ol, other0)

time: 53.8 us -> 49.7 us (0.924)
  waiting for transfers between devices: 19.2 us -> 11.9 us
  starting transfers between devices: 12.6 us -> 16.2 us
  local copies, waits for them, and re-layouts: 1.41 us -> 0.78 us
    ppermute x8, waiting for transfers between devices: 19.2 us -> 11.9 us  [route(): return lax.ppermute(a, ('seq', 'head'), pairs)]
    ppermute x8, starting transfers between devices: 12.6 us -> 16.2 us  [route(): return lax.ppermute(a, ('seq', 'head'), pairs)]
    add x1, other arithmetic: 0.05 us -> 0.82 us  [body(): other = partner(keep[:STATE] + keep[STATE:STATE + 1] * mine)]
    slice x1 -> x0, other arithmetic: 0.75 us -> none  [body(): fade = got[STATE:STATE + 1] * keep[STATE:STATE + 1]]
    unnamed x10 -> x8, local copies, waits for them, and re-layouts: 1.41 us -> 0.74 us
    add x2 -> x1, other arithmetic: 1.05 us -> 1.09 us  [body(): chip = jnp.where(row < STATE, got, 0.0) + got[STATE:STATE + 1] * keep]
  transfers between devices with their start and end apart: 8 -> 8, of which waited for: 5 -> 4; matrix products, arithmetic and copies ran while one was open for 0% -> 0% of each run, Pallas kernels for 24% -> 27%
where the time goes in v4:
time: 49.7 us; the launch traced here: 49.2 us
  Pallas kernels  16.9 us (34%)
  starting transfers between devices  16.2 us (33%)
  waiting for transfers between devices  11.9 us (24%)
  other arithmetic  2.68 us (5%)
  local copies, waits for them, and re-layouts  0.78 us (2%)
  between operations  0.71 us (1%)
    pallas_call x5, Pallas kernels, call(): pl.pallas_call(kernel, name=name, out_shape=[jax.ShapeDtypeStruct(s, d) f...  16.9 us
    ppermute x8, starting transfers between devices, route(): return lax.ppermute(a, ('seq', 'head'), pairs)  16.2 us
    ppermute x8, waiting for transfers between devices, route(): return lax.ppermute(a, ('seq', 'head'), pairs)  11.9 us
    add x1, other arithmetic, body(): chip = jnp.where(row < STATE, got, 0.0) + got[STATE:STATE + 1] * keep  1.09 us
  transfers between devices with their start and end apart: 8, of which 4 were waited for; matrix products, arithmetic and copies ran while one was open for 0% of the time, Pallas kernels for 27%

profile of v4, /device:TPU:6, one launch (start us, length us, event | category | flops | bytes accessed | tf_op | source)
XLA Modules:
  0.0 49.2 jit_solution(10866902580655449806)
XLA Ops:
  0.6 3.8 %edges.1 = (f32[136,640]{1,0:T(8,128)}, f32[136,640]{1,0:T(8,128)}, bf16[256,640]{1,0:T(8,128)(2,1)}, bf16[256,640]{1,0:T(8,128)(2,1)}, bf16[256,640]{1,0:T(8,12...) custom-call(s32[1]{0:T(128)} %bitcast.place, ...), custom_call_target="tpu_custom_call" | custom-call | tf_op jit(solution)/shard_map/edges/pallas_call | solution.py:179
  4.5 0.1 collective-permute-start
  4.6 1.8 %collective-permute-done = f32[136,640]{1,0:T(8,128)S(1)} collective-permute-done((f32[136,640]{1,0:T(8,128)}, f32[136,640]{1,0:T(8,128)S(1)}, u32[]{:S(2)}, u32[]{:S(2)}) %collective-permute-start) | collective-permute-done | bytes 348192 | tf_op jit(solution)/shard_map/ppermute | solution.py:196
  6.5 1.1 %multiply_add_fusion = f32[136,640]{1,0:T(8,128)S(1)} fusion(f32[136,640]{1,0:T(8,128)} %get-tuple-element.24, f32[136,640]{1,0:T(8,128)S(1)} %collective-permute-done, f32[640]{0:T(1024)S(1)} %slice_reduce_fusion, pred[136]{0:T(512)(128)(4,1)S(1)} %iota_compare_fusion), kind=kLoop, calls=%fused_computation | loop fusion | flops 261120 | bytes 1047176 | tf_op jit(solution)/shard_map/add | solution.py:221
  7.5 3.8 %collective-permute-start.1 = (f32[136,640]{1,0:T(8,128)S(1)}, f32[136,640]{1,0:T(8,128)S(1)}, u32[]{:S(2)}, u32[]{:S(2)}) collective-permute-start(f32[136,640]{1,0:T(8,128)S(1)} %multiply_add_fusion), channel_id=1, source_target_pairs={{0,8},{1,9},{2,10},{3,11},{8,16},{9,17},{10,18},{11,19},{12,4},{13... | collective-permute-start | bytes 1044488 | tf_op jit(solution)/shard_map/ppermute | solution.py:196
  11.4 5.2 %collective-permute-start.2 = (f32[136,640]{1,0:T(8,128)S(1)}, f32[136,640]{1,0:T(8,128)S(1)}, u32[]{:S(2)}, u32[]{:S(2)}) collective-permute-start(f32[136,640]{1,0:T(8,128)S(1)} %multiply_add_fusion), channel_id=1, source_target_pairs={{0,16},{1,17},{2,18},{3,19},{8,24},{9,25},{10,26},{11,27},{16,32},... | collective-permute-start | bytes 1044488 | tf_op jit(solution)/shard_map/ppermute | solution.py:196
  16.6 0.0 copy-start
  16.6 5.0 %local.1 = (f32[256,640]{1,0:T(8,128)}, f32[256,640]{1,0:T(8,128)}, f32[256,128]{1,0:T(8,128)}, f32[256,128]{1,0:T(8,128)}) custom-call(s32[1]{0:T(128)} %bitcast.place, f32[10]{0:T(128)} %skips.1, f32[256,20]{1,0:T(8,128)} %get-tuple-element.25.facts, f32[256,8]{1,0:T(8,128)} %get-tuple-element.26.segs, f32[8,256]{1,0:T(8,128)} %get-tuple-element.27.segr, ...), custom_call_target="tpu_custom_call" | custom-call | tf_op jit(solution)/shard_map/local/pallas_call | solution.py:179
  21.6 0.0 copy-done
  21.6 0.0 collective-permute-done.1
  21.6 6.8 %collective-permute-done.2 = f32[136,640]{1,0:T(8,128)S(1)} collective-permute-done((f32[136,640]{1,0:T(8,128)S(1)}, f32[136,640]{1,0:T(8,128)S(1)}, u32[]{:S(2)}, u32[]{:S(2)}) %collective-permute-start.2) | collective-permute-done | bytes 348192 | tf_op jit(solution)/shard_map/ppermute | solution.py:196
  28.4 0.8 %multiply_add_fusion.1 = (f32[128,640]{1,0:T(8,128)S(1)}, f32[128,640]{1,0:T(8,128)}) fusion(f32[136,640]{1,0:T(8,128)S(1)} %copy-done, f32[640]{0:T(1024)S(1)} %slice_reduce_fusion.1, f32[136,640]{1,0:T(8,128)S(1)} %collective-permute-done.2, f32[640]{0:T(1024)S(1)} %slice_reduce_fusion.2, f32[136,640]{1,0:T(8,128)S(1)} %collective-permute-done.1), kind=kLoop, calls=%fused_computation.1 | loop fusion | flops 327680 | bytes 1643520 | tf_op jit(solution)/shard_map/add | solution.py:230
  29.3 0.0 collective-permute-start.3
  29.3 2.3 %first.1 = f32[256,128]{1,0:T(8,128)} custom-call(s32[1]{0:T(128)} %bitcast.place, f32[128,640]{1,0:T(8,128)} %get-tuple-element.43.mine.state, f32[8,640]{1,0:T(8,128)} %get-tuple-element.35.last, f32[256,8]{1,0:T(8,128)} %get-tuple-element.26.segs, bf16[256,640]{1,0:T(8,128)(2,1)} %get-tuple-element.28.mh.high, bf16[256,640]{1,0:T(8,128)(2,1)} %get-tuple-element.29.ml.low, ...), custom_call_target="tpu_custom_call" | custom-call | tf_op jit(solution)/shard_map/first/pallas_call | solution.py:179
  31.6 1.6 %collective-permute-start.6 = (f32[256,128]{1,0:T(8,128)}, f32[256,128]{1,0:T(8,128)S(1)}, u32[]{:S(2)}, u32[]{:S(2)}) collective-permute-start(f32[256,128]{1,0:T(8,128)} %first.1), channel_id=1, source_target_pairs={{0,1},{1,0},{2,3},{3,2},{4,7},{5,6},{6,5},{7,4},{8,9},{9,8},{10,11... | collective-permute-start | bytes 393224 | tf_op jit(solution)/shard_map/ppermute | solution.py:196
  33.2 0.0 collective-permute-done.3.other.state
  33.2 0.0 copy-start.1
  33.2 0.7 %copy-done.1 = f32[128,640]{1,0:T(8,128)} copy-done((f32[128,640]{1,0:T(8,128)}, f32[128,640]{1,0:T(8,128)S(1)}, u32[]{:S(2)}) %copy-start.1) | copy-done | bytes 327704
  33.9 0.0 copy-start.2
  33.9 2.4 %second.1 = f32[256,128]{1,0:T(8,128)} custom-call(s32[1]{0:T(128)} %bitcast.place, f32[128,640]{1,0:T(8,128)} %copy-done.1, f32[8,640]{1,0:T(8,128)} %get-tuple-element.35.last, f32[256,8]{1,0:T(8,128)} %get-tuple-element.26.segs, bf16[256,640]{1,0:T(8,128)(2,1)} %get-tuple-element.30.oh.high, bf16[256,640]{1,0:T(8,128)(2,1)} %get-tuple-element.31.ol.low, ...), custom_call_target="tpu_custom_call" | custom-call | tf_op jit(solution)/shard_map/second/pallas_call | solution.py:179
  36.3 0.0 copy-start.3
  36.3 0.4 collective-permute-start.4
  36.8 0.0 collective-permute-done.6
  36.8 0.0 copy-done.2
  36.8 3.3 %collective-permute-start.7 = (f32[256,128]{1,0:T(8,128)S(1)}, f32[256,128]{1,0:T(8,128)S(1)}, u32[]{:S(2)}, u32[]{:S(2)}) collective-permute-start(f32[256,128]{1,0:T(8,128)S(1)} %add.26), channel_id=1, source_target_pairs={{0,3},{1,2},{2,1},{3,0},{4,5},{5,4},{6,7},{7,6},{8,11},{9,10},{10,... | collective-permute-start | bytes 393224 | tf_op jit(solution)/shard_map/ppermute | solution.py:196
  40.1 2.1 %collective-permute-done.4 = f32[256,128]{1,0:T(8,128)S(1)} collective-permute-done((f32[256,128]{1,0:T(8,128)}, f32[256,128]{1,0:T(8,128)S(1)}, u32[]{:S(2)}, u32[]{:S(2)}) %collective-permute-start.4) | collective-permute-done | bytes 131104 | tf_op jit(solution)/shard_map/ppermute | solution.py:196
  42.2 0.0 copy-done.3
  42.2 1.8 %collective-permute-start.5 = (f32[256,128]{1,0:T(8,128)S(1)}, f32[256,128]{1,0:T(8,128)S(1)}, u32[]{:S(2)}, u32[]{:S(2)}) collective-permute-start(f32[256,128]{1,0:T(8,128)S(1)} %add.24), channel_id=1, source_target_pairs={{0,3},{1,2},{2,1},{3,0},{4,5},{5,4},{6,7},{7,6},{8,11},{9,10},{10,... | collective-permute-start | bytes 393224 | tf_op jit(solution)/shard_map/ppermute | solution.py:196
  44.0 3.3 %outs.1 = (bf16[256,640]{1,0:T(8,128)(2,1)}, bf16[256,640]{1,0:T(8,128)(2,1)}) custom-call(s32[1]{0:T(128)} %bitcast.place, f32[128,640]{1,0:T(8,128)} %get-tuple-element.43.mine.state, f32[128,640]{1,0:T(8,128)} %copy-done.1, f32[8,640]{1,0:T(8,128)} %get-tuple-element.35.last, f32[256,20]{1,0:T(8,128)} %get-tuple-element.25.facts, ...), custom_call_target="tpu_custom_call" | custom-call | tf_op jit(solution)/shard_map/outs/pallas_call | solution.py:179
  47.3 0.0 collective-permute-done.7
  47.3 1.1 %collective-permute-done.5 = f32[256,128]{1,0:T(8,128)S(1)} collective-permute-done((f32[256,128]{1,0:T(8,128)S(1)}, f32[256,128]{1,0:T(8,128)S(1)}, u32[]{:S(2)}, u32[]{:S(2)}) %collective-permute-start.5) | collective-permute-done | bytes 131104 | tf_op jit(solution)/shard_map/ppermute | solution.py:196
  48.5 0.7 %broadcast_select_fusion = (f32[256,128]{1,0:T(8,128)}, f32[256,128]{1,0:T(8,128)}) fusion(pred[]{:T(512)S(6)} %eq.3, f32[256,128]{1,0:T(8,128)S(1)} %add.26, f32[256,128]{1,0:T(8,128)S(1)} %collective-permute-done.7, f32[256,128]{1,0:T(8,128)S(1)} %add.24, f32[256,128]{1,0:T(8,128)S(1)} %collective-permute-done.5), kind=kLoop, calls=%fused_computation.3 | loop fusion | flops 131072 | bytes 786433 | tf_op jit(solution)/shard_map/jit(_where)/select_n | solution.py:239
  (6 shorter events, 0.1 us)
Async XLA Ops:
  4.5 2.0 %collective-permute-start = (f32[136,640]{1,0:T(8,128)}, f32[136,640]{1,0:T(8,128)S(1)}, u32[]{:S(2)}, u32[]{:S(2)}) collective-permute-start(f32[136,640]{1,0:T(8,128)} %get-tuple-element.23), channel_id=1, source_target_pairs={{0,4},{1,5},{2,6},{3,7},{4,0},{5,1},{6,2},{7,3},{8,12},{9,13},{10,... | collective-permute-start | bytes 1044488 | tf_op jit(solution)/shard_map/ppermute | solution.py:196
  7.5 14.1 %collective-permute-start.1 = (f32[136,640]{1,0:T(8,128)S(1)}, f32[136,640]{1,0:T(8,128)S(1)}, u32[]{:S(2)}, u32[]{:S(2)}) collective-permute-start(f32[136,640]{1,0:T(8,128)S(1)} %multiply_add_fusion), channel_id=1, source_target_pairs={{0,8},{1,9},{2,10},{3,11},{8,16},{9,17},{10,18},{11,19},{12,4},{13... | collective-permute-start | bytes 1044488 | tf_op jit(solution)/shard_map/ppermute | solution.py:196
  11.4 17.1 %collective-permute-start.2 = (f32[136,640]{1,0:T(8,128)S(1)}, f32[136,640]{1,0:T(8,128)S(1)}, u32[]{:S(2)}, u32[]{:S(2)}) collective-permute-start(f32[136,640]{1,0:T(8,128)S(1)} %multiply_add_fusion), channel_id=1, source_target_pairs={{0,16},{1,17},{2,18},{3,19},{8,24},{9,25},{10,26},{11,27},{16,32},... | collective-permute-start | bytes 1044488 | tf_op jit(solution)/shard_map/ppermute | solution.py:196
  16.6 5.0 %copy-start = (f32[136,640]{1,0:T(8,128)S(1)}, f32[136,640]{1,0:T(8,128)}, u32[]{:S(2)}) copy-start(f32[136,640]{1,0:T(8,128)} %get-tuple-element.24) | copy-start | bytes 1044484
  29.3 3.9 %collective-permute-start.3 = (f32[128,640]{1,0:T(8,128)S(1)}, f32[128,640]{1,0:T(8,128)S(1)}, u32[]{:S(2)}, u32[]{:S(2)}) collective-permute-start(f32[128,640]{1,0:T(8,128)S(1)} %get-tuple-element.42), channel_id=1, source_target_pairs={{0,4},{1,5},{2,6},{3,7},{4,0},{5,1},{6,2},{7,3},{8,12},{9,13},{10,... | collective-permute-start | bytes 983048 | tf_op jit(solution)/shard_map/ppermute | solution.py:196
  31.6 5.2 %collective-permute-start.6 = (f32[256,128]{1,0:T(8,128)}, f32[256,128]{1,0:T(8,128)S(1)}, u32[]{:S(2)}, u32[]{:S(2)}) collective-permute-start(f32[256,128]{1,0:T(8,128)} %first.1), channel_id=1, source_target_pairs={{0,1},{1,0},{2,3},{3,2},{4,7},{5,6},{6,5},{7,4},{8,9},{9,8},{10,11... | collective-permute-start | bytes 393224 | tf_op jit(solution)/shard_map/ppermute | solution.py:196
  33.2 0.7 %copy-start.1 = (f32[128,640]{1,0:T(8,128)}, f32[128,640]{1,0:T(8,128)S(1)}, u32[]{:S(2)}) copy-start(f32[128,640]{1,0:T(8,128)S(1)} %collective-permute-done.3.other.state) | copy-start | bytes 983044
  33.9 2.9 %copy-start.2 = (f32[256,128]{1,0:T(8,128)S(1)}, f32[256,128]{1,0:T(8,128)}, u32[]{:S(2)}) copy-start(f32[256,128]{1,0:T(8,128)} %first.1) | copy-start | bytes 393220
  36.3 5.8 %copy-start.3 = (f32[256,128]{1,0:T(8,128)S(1)}, f32[256,128]{1,0:T(8,128)}, u32[]{:S(2)}) copy-start(f32[256,128]{1,0:T(8,128)} %second.1) | copy-start | bytes 393220
  36.3 5.8 %collective-permute-start.4 = (f32[256,128]{1,0:T(8,128)}, f32[256,128]{1,0:T(8,128)S(1)}, u32[]{:S(2)}, u32[]{:S(2)}) collective-permute-start(f32[256,128]{1,0:T(8,128)} %second.1), channel_id=1, source_target_pairs={{0,1},{1,0},{2,3},{3,2},{4,7},{5,6},{6,5},{7,4},{8,9},{9,8},{10,11... | collective-permute-start | bytes 393224 | tf_op jit(solution)/shard_map/ppermute | solution.py:196
  36.8 10.5 %collective-permute-start.7 = (f32[256,128]{1,0:T(8,128)S(1)}, f32[256,128]{1,0:T(8,128)S(1)}, u32[]{:S(2)}, u32[]{:S(2)}) collective-permute-start(f32[256,128]{1,0:T(8,128)S(1)} %add.26), channel_id=1, source_target_pairs={{0,3},{1,2},{2,1},{3,0},{4,5},{5,4},{6,7},{7,6},{8,11},{9,10},{10,... | collective-permute-start | bytes 393224 | tf_op jit(solution)/shard_map/ppermute | solution.py:196
  42.2 6.3 %collective-permute-start.5 = (f32[256,128]{1,0:T(8,128)S(1)}, f32[256,128]{1,0:T(8,128)S(1)}, u32[]{:S(2)}, u32[]{:S(2)}) collective-permute-start(f32[256,128]{1,0:T(8,128)S(1)} %add.24), channel_id=1, source_target_pairs={{0,3},{1,2},{2,1},{3,0},{4,5},{5,4},{6,7},{7,6},{8,11},{9,10},{10,... | collective-permute-start | bytes 393224 | tf_op jit(solution)/shard_map/ppermute | solution.py:196

commit v5 on v4

--- a/solution.py
+++ b/solution.py
@@ -68,7 +68,7 @@
     return out
 
 
-def edge_kernel(place, rates, docs, dt, x, g, b, c, send, keep, mh, ml, oh, ol, facts, segs, segr, last):
+def edge_kernel(place, rates, docs, dt, x, g, b, c, send, keep, facts, segs, segr, last):
     length, width = x.shape
     heads = dt.shape[0]
     core = place[0] % 2
@@ -104,17 +104,6 @@
     x_parts = halves(x[...] * shrink_x)
     g_parts = halves(g[...] * grow_x)
     is_zero = core == 0
-
-    @pl.when(is_zero)
-    def _():
-        mh[...], ml[...] = g_parts
-        oh[...], ol[...] = x_parts
-
-    @pl.when(core == 1)
-    def _():
-        mh[...], ml[...] = x_parts
-        oh[...], ol[...] = g_parts
-
     b_parts = halves((b[...] * final).T)
     c_parts = halves((c[...] * entry).T)
     end = dot3(b_parts, x_parts, NN) * total
@@ -127,7 +116,7 @@
     keep[STATE:, :] = whole
 
 
-def local_kernel(place, skips, facts, segs, segr, x, g, mh, ml, oh, ol, b, c, y0, z0, mine, other):
+def local_kernel(place, skips, facts, segs, segr, x, g, b, c, y0, z0, mine, other, mh, ml, oh, ol):
     length, width = x.shape
     heads = facts.shape[1] // 2
     b_parts = halves(b[...])
@@ -138,15 +127,19 @@
     mask = jnp.where(same & (s_at <= t_at), 1.0, 0.0)
     mask_t = jnp.where(same & (t_at <= s_at), 1.0, 0.0)
     core = place[0] % 2
-    m_parts = (mh[...], ml[...])
-    o_parts = (oh[...], ol[...])
-    x_parts = [jnp.where(core == 0, o, m) for m, o in zip(m_parts, o_parts)]
-    g_parts = [jnp.where(core == 0, m, o) for m, o in zip(m_parts, o_parts)]
+    grow_x = spread(facts[:, :heads], heads, width)
+    shrink_x = spread(facts[:, heads:], heads, width)
+    x_parts = halves(x[...] * shrink_x)
+    g_parts = halves(g[...] * grow_x)
+    mh[...] = jnp.where(core == 0, g_parts[0], x_parts[0])
+    ml[...] = jnp.where(core == 0, g_parts[1], x_parts[1])
+    oh[...] = jnp.where(core == 0, x_parts[0], g_parts[0])
+    ol[...] = jnp.where(core == 0, x_parts[1], g_parts[1])
     mix = halves(dot3(c_parts, b_parts, NT) * mask)
     mix_t = halves(dot3(b_parts, c_parts, NT) * mask_t)
     skip = head_row(skips, heads, width)
-    y0[...] = dot3(mix, x_parts, NN) * spread(facts[:, :heads], heads, width) + skip * x[...]
-    z0[...] = dot3(mix_t, g_parts, NN) * spread(facts[:, heads:], heads, width) + skip * g[...]
+    y0[...] = dot3(mix, x_parts, NN) * grow_x + skip * x[...]
+    z0[...] = dot3(mix_t, g_parts, NN) * shrink_x + skip * g[...]
     weight = dot3(g_parts, x_parts, NT) * mask
     grad_b = dot3(halves(weight.T), c_parts, NN)
     grad_c = dot3(halves(weight), b_parts, NN)
@@ -211,9 +204,9 @@
         place = lax.axis_index("seq").astype(jnp.int32).reshape(1)
         state = (STATE + 8, width)
         wide = (length, width)
-        send, keep, mh, ml, oh, ol, facts, segs, segr, last = call(
+        send, keep, facts, segs, segr, last = call(
             edge_kernel, "edges",
-            [(state, f32), (state, f32), (wide, bf16), (wide, bf16), (wide, bf16), (wide, bf16),
+            [(state, f32), (state, f32),
              ((length, 2 * heads), f32), ((length, 8), f32), ((8, length), f32), ((8, width), f32)],
             (0, 1), place, rates, docs.reshape(1, -1), dt, x, g, b, c)
         got = partner(send)
@@ -222,9 +215,9 @@
         far = chips(chip, 2)
         near = chips(chip, 1)
         thin = ((length, STATE), f32)
-        y0, z0, mine0, other0 = call(
-            local_kernel, "local", [(wide, f32), (wide, f32), thin, thin],
-            (0, 1), place, skips, facts, segs, segr, x, g, mh, ml, oh, ol, b, c)
+        y0, z0, mine0, other0, mh, ml, oh, ol = call(
+            local_kernel, "local", [(wide, f32), (wide, f32), thin, thin] + 4 * [(wide, bf16)],
+            (0, 1), place, skips, facts, segs, segr, x, g, b, c)
         near, far, mine0 = lax.optimization_barrier((near, far, mine0))
         mine = near[:STATE] + near[STATE : STATE + 1] * far[:STATE]
         other = partner(keep[:STATE] + keep[STATE : STATE + 1] * mine)

time: 49.7 us -> 49.3 us (level)
  waiting for transfers between devices: 11.9 us -> 12.8 us
  Pallas kernels: 16.9 us -> 16.3 us
  starting transfers between devices: 16.2 us -> 15.7 us
    ppermute x8, waiting for transfers between devices: 11.9 us -> 12.8 us  [route(): return lax.ppermute(a, ('seq', 'head'), pairs)]
    pallas_call x5, Pallas kernels: 16.9 us -> 16.3 us  [call(): pl.pallas_call(kernel, name=name, out_shape=[jax.ShapeDtypeStruct(s, d) f...]
  transfers between devices with their start and end apart: 8 -> 8, of which waited for: 4 -> 4; matrix products, arithmetic and copies ran while one was open for 0% -> 0% of each run, Pallas kernels for 27% -> 26%
where the time goes in v5:
time: 49.3 us; the launch traced here: 49 us
  Pallas kernels  16.3 us (33%)
  starting transfers between devices  15.7 us (32%)
  waiting for transfers between devices  12.8 us (26%)
  other arithmetic  2.68 us (5%)
  local copies, waits for them, and re-layouts  0.78 us (2%)
  between operations  0.71 us (1%)
    pallas_call x5, Pallas kernels, call(): pl.pallas_call(kernel, name=name, out_shape=[jax.ShapeDtypeStruct(s, d) f...  16.3 us
    ppermute x8, starting transfers between devices, route(): return lax.ppermute(a, ('seq', 'head'), pairs)  15.7 us
    ppermute x8, waiting for transfers between devices, route(): return lax.ppermute(a, ('seq', 'head'), pairs)  12.8 us
    add x1, other arithmetic, body(): chip = jnp.where(row < STATE, got, 0.0) + got[STATE:STATE + 1] * keep  1.09 us
  transfers between devices with their start and end apart: 8, of which 4 were waited for; matrix products, arithmetic and copies ran while one was open for 0% of the time, Pallas kernels for 26%

profile of v5, /device:TPU:6, one launch (start us, length us, event | category | flops | bytes accessed | tf_op | source)
XLA Modules:
  0.0 49.0 jit_solution(9779266302687305059)
XLA Ops:
  0.6 3.5 %edges.1 = (f32[136,640]{1,0:T(8,128)}, f32[136,640]{1,0:T(8,128)}, f32[256,20]{1,0:T(8,128)}, f32[256,8]{1,0:T(8,128)}, f32[8,256]{1,0:T(8,128)}, /*index=5*/f32[8,640]{1,0:T(8,128)}) custom-call(s32[1]{0:T(128)} %bitcast.place, f32[10]{0:T(128)} %rates.1, s32[1,128]{1,0:T(1,128)} %bitcast.2, f32[10,256]{1,0:T(8,128)} %dt.1, f32[256,640]{1,0:T(8,128)} %x.3, ...), custom_call_target="tpu_custom_call" | custom-call | tf_op jit(solution)/shard_map/edges/pallas_call | solution.py:172
  4.1 0.0 collective-permute-start
  4.1 1.8 %collective-permute-done = f32[136,640]{1,0:T(8,128)S(1)} collective-permute-done((f32[136,640]{1,0:T(8,128)}, f32[136,640]{1,0:T(8,128)S(1)}, u32[]{:S(2)}, u32[]{:S(2)}) %collective-permute-start) | collective-permute-done | bytes 348192 | tf_op jit(solution)/shard_map/ppermute | solution.py:189
  6.0 1.1 %multiply_add_fusion = f32[136,640]{1,0:T(8,128)S(1)} fusion(f32[136,640]{1,0:T(8,128)} %get-tuple-element.24, f32[136,640]{1,0:T(8,128)S(1)} %collective-permute-done, f32[640]{0:T(1024)S(1)} %slice_reduce_fusion, pred[136]{0:T(512)(128)(4,1)S(1)} %iota_compare_fusion), kind=kLoop, calls=%fused_computation | loop fusion | flops 261120 | bytes 1047176 | tf_op jit(solution)/shard_map/add | solution.py:214
  7.1 3.8 %collective-permute-start.1 = (f32[136,640]{1,0:T(8,128)S(1)}, f32[136,640]{1,0:T(8,128)S(1)}, u32[]{:S(2)}, u32[]{:S(2)}) collective-permute-start(f32[136,640]{1,0:T(8,128)S(1)} %multiply_add_fusion), channel_id=1, source_target_pairs={{0,8},{1,9},{2,10},{3,11},{8,16},{9,17},{10,18},{11,19},{12,4},{13... | collective-permute-start | bytes 1044488 | tf_op jit(solution)/shard_map/ppermute | solution.py:189
  10.9 5.2 %collective-permute-start.2 = (f32[136,640]{1,0:T(8,128)S(1)}, f32[136,640]{1,0:T(8,128)S(1)}, u32[]{:S(2)}, u32[]{:S(2)}) collective-permute-start(f32[136,640]{1,0:T(8,128)S(1)} %multiply_add_fusion), channel_id=1, source_target_pairs={{0,16},{1,17},{2,18},{3,19},{8,24},{9,25},{10,26},{11,27},{16,32},... | collective-permute-start | bytes 1044488 | tf_op jit(solution)/shard_map/ppermute | solution.py:189
  16.1 0.0 copy-start
  16.1 4.8 %local.1 = (f32[256,640]{1,0:T(8,128)}, f32[256,640]{1,0:T(8,128)}, f32[256,128]{1,0:T(8,128)}, f32[256,128]{1,0:T(8,128)}, bf16[256,640]{1,0:T(8,128)(2,1)}, /*...) custom-call(s32[1]{0:T(128)} %bitcast.place, f32[10]{0:T(128)} %skips.1, ...), custom_call_target="tpu_custom_call" | custom-call | tf_op jit(solution)/shard_map/local/pallas_call | solution.py:172
  20.9 0.0 copy-done
  20.9 0.0 collective-permute-done.1
  20.9 7.1 %collective-permute-done.2 = f32[136,640]{1,0:T(8,128)S(1)} collective-permute-done((f32[136,640]{1,0:T(8,128)S(1)}, f32[136,640]{1,0:T(8,128)S(1)}, u32[]{:S(2)}, u32[]{:S(2)}) %collective-permute-start.2) | collective-permute-done | bytes 348192 | tf_op jit(solution)/shard_map/ppermute | solution.py:189
  28.0 0.8 %multiply_add_fusion.1 = (f32[128,640]{1,0:T(8,128)S(1)}, f32[128,640]{1,0:T(8,128)}) fusion(f32[136,640]{1,0:T(8,128)S(1)} %copy-done, f32[640]{0:T(1024)S(1)} %slice_reduce_fusion.1, f32[136,640]{1,0:T(8,128)S(1)} %collective-permute-done.2, f32[640]{0:T(1024)S(1)} %slice_reduce_fusion.2, f32[136,640]{1,0:T(8,128)S(1)} %collective-permute-done.1), kind=kLoop, calls=%fused_computation.1 | loop fusion | flops 327680 | bytes 1643520 | tf_op jit(solution)/shard_map/add | solution.py:223
  28.8 0.0 collective-permute-start.3
  28.8 2.3 %first.1 = f32[256,128]{1,0:T(8,128)} custom-call(s32[1]{0:T(128)} %bitcast.place, f32[128,640]{1,0:T(8,128)} %get-tuple-element.43.mine.state, f32[8,640]{1,0:T(8,128)} %get-tuple-element.31.last, f32[256,8]{1,0:T(8,128)} %get-tuple-element.26.segs, bf16[256,640]{1,0:T(8,128)(2,1)} %get-tuple-element.39.high, bf16[256,640]{1,0:T(8,128)(2,1)} %get-tuple-element.40.low, ...), custom_call_target="tpu_custom_call" | custom-call | tf_op jit(solution)/shard_map/first/pallas_call | solution.py:172
  31.1 1.7 %collective-permute-start.6 = (f32[256,128]{1,0:T(8,128)}, f32[256,128]{1,0:T(8,128)S(1)}, u32[]{:S(2)}, u32[]{:S(2)}) collective-permute-start(f32[256,128]{1,0:T(8,128)} %first.1), channel_id=1, source_target_pairs={{0,1},{1,0},{2,3},{3,2},{4,7},{5,6},{6,5},{7,4},{8,9},{9,8},{10,11... | collective-permute-start | bytes 393224 | tf_op jit(solution)/shard_map/ppermute | solution.py:189
  32.8 0.0 collective-permute-done.3.other.state
  32.8 0.0 copy-start.1
  32.8 0.7 %copy-done.1 = f32[128,640]{1,0:T(8,128)} copy-done((f32[128,640]{1,0:T(8,128)}, f32[128,640]{1,0:T(8,128)S(1)}, u32[]{:S(2)}) %copy-start.1) | copy-done | bytes 327704
  33.6 0.0 copy-start.2
  33.6 2.4 %second.1 = f32[256,128]{1,0:T(8,128)} custom-call(s32[1]{0:T(128)} %bitcast.place, f32[128,640]{1,0:T(8,128)} %copy-done.1, f32[8,640]{1,0:T(8,128)} %get-tuple-element.31.last, f32[256,8]{1,0:T(8,128)} %get-tuple-element.26.segs, bf16[256,640]{1,0:T(8,128)(2,1)} %get-tuple-element.36.high, bf16[256,640]{1,0:T(8,128)(2,1)} %get-tuple-element.37.low, ...), custom_call_target="tpu_custom_call" | custom-call | tf_op jit(solution)/shard_map/second/pallas_call | solution.py:172
  36.0 0.0 copy-start.3
  36.0 0.3 collective-permute-start.4
  36.3 0.0 collective-permute-done.6
  36.3 0.0 copy-done.2
  36.4 3.2 %collective-permute-start.7 = (f32[256,128]{1,0:T(8,128)S(1)}, f32[256,128]{1,0:T(8,128)S(1)}, u32[]{:S(2)}, u32[]{:S(2)}) collective-permute-start(f32[256,128]{1,0:T(8,128)S(1)} %add.26), channel_id=1, source_target_pairs={{0,3},{1,2},{2,1},{3,0},{4,5},{5,4},{6,7},{7,6},{8,11},{9,10},{10,... | collective-permute-start | bytes 393224 | tf_op jit(solution)/shard_map/ppermute | solution.py:189
  39.6 2.4 %collective-permute-done.4 = f32[256,128]{1,0:T(8,128)S(1)} collective-permute-done((f32[256,128]{1,0:T(8,128)}, f32[256,128]{1,0:T(8,128)S(1)}, u32[]{:S(2)}, u32[]{:S(2)}) %collective-permute-start.4) | collective-permute-done | bytes 131104 | tf_op jit(solution)/shard_map/ppermute | solution.py:189
  42.0 0.0 copy-done.3
  42.0 1.5 %collective-permute-start.5 = (f32[256,128]{1,0:T(8,128)S(1)}, f32[256,128]{1,0:T(8,128)S(1)}, u32[]{:S(2)}, u32[]{:S(2)}) collective-permute-start(f32[256,128]{1,0:T(8,128)S(1)} %add.24), channel_id=1, source_target_pairs={{0,3},{1,2},{2,1},{3,0},{4,5},{5,4},{6,7},{7,6},{8,11},{9,10},{10,... | collective-permute-start | bytes 393224 | tf_op jit(solution)/shard_map/ppermute | solution.py:189
  43.5 3.3 %outs.1 = (bf16[256,640]{1,0:T(8,128)(2,1)}, bf16[256,640]{1,0:T(8,128)(2,1)}) custom-call(s32[1]{0:T(128)} %bitcast.place, f32[128,640]{1,0:T(8,128)} %get-tuple-element.43.mine.state, f32[128,640]{1,0:T(8,128)} %copy-done.1, f32[8,640]{1,0:T(8,128)} %get-tuple-element.31.last, f32[256,20]{1,0:T(8,128)} %get-tuple-element.25.facts, ...), custom_call_target="tpu_custom_call" | custom-call | tf_op jit(solution)/shard_map/outs/pallas_call | solution.py:172
  46.8 0.0 collective-permute-done.7
  46.8 1.5 %collective-permute-done.5 = f32[256,128]{1,0:T(8,128)S(1)} collective-permute-done((f32[256,128]{1,0:T(8,128)S(1)}, f32[256,128]{1,0:T(8,128)S(1)}, u32[]{:S(2)}, u32[]{:S(2)}) %collective-permute-start.5) | collective-permute-done | bytes 131104 | tf_op jit(solution)/shard_map/ppermute | solution.py:189
  48.3 0.7 %broadcast_select_fusion = (f32[256,128]{1,0:T(8,128)}, f32[256,128]{1,0:T(8,128)}) fusion(pred[]{:T(512)S(6)} %eq.3, f32[256,128]{1,0:T(8,128)S(1)} %add.26, f32[256,128]{1,0:T(8,128)S(1)} %collective-permute-done.7, f32[256,128]{1,0:T(8,128)S(1)} %add.24, f32[256,128]{1,0:T(8,128)S(1)} %collective-permute-done.5), kind=kLoop, calls=%fused_computation.3 | loop fusion | flops 131072 | bytes 786433 | tf_op jit(solution)/shard_map/jit(_where)/select_n | solution.py:232
  (6 shorter events, 0.1 us)
Async XLA Ops:
  4.1 1.9 %collective-permute-start = (f32[136,640]{1,0:T(8,128)}, f32[136,640]{1,0:T(8,128)S(1)}, u32[]{:S(2)}, u32[]{:S(2)}) collective-permute-start(f32[136,640]{1,0:T(8,128)} %get-tuple-element.23), channel_id=1, source_target_pairs={{0,4},{1,5},{2,6},{3,7},{4,0},{5,1},{6,2},{7,3},{8,12},{9,13},{10,... | collective-permute-start | bytes 1044488 | tf_op jit(solution)/shard_map/ppermute | solution.py:189
  7.1 13.8 %collective-permute-start.1 = (f32[136,640]{1,0:T(8,128)S(1)}, f32[136,640]{1,0:T(8,128)S(1)}, u32[]{:S(2)}, u32[]{:S(2)}) collective-permute-start(f32[136,640]{1,0:T(8,128)S(1)} %multiply_add_fusion), channel_id=1, source_target_pairs={{0,8},{1,9},{2,10},{3,11},{8,16},{9,17},{10,18},{11,19},{12,4},{13... | collective-permute-start | bytes 1044488 | tf_op jit(solution)/shard_map/ppermute | solution.py:189
  10.9 17.1 %collective-permute-start.2 = (f32[136,640]{1,0:T(8,128)S(1)}, f32[136,640]{1,0:T(8,128)S(1)}, u32[]{:S(2)}, u32[]{:S(2)}) collective-permute-start(f32[136,640]{1,0:T(8,128)S(1)} %multiply_add_fusion), channel_id=1, source_target_pairs={{0,16},{1,17},{2,18},{3,19},{8,24},{9,25},{10,26},{11,27},{16,32},... | collective-permute-start | bytes 1044488 | tf_op jit(solution)/shard_map/ppermute | solution.py:189
  16.1 4.8 %copy-start = (f32[136,640]{1,0:T(8,128)S(1)}, f32[136,640]{1,0:T(8,128)}, u32[]{:S(2)}) copy-start(f32[136,640]{1,0:T(8,128)} %get-tuple-element.24) | copy-start | bytes 1044484
  28.8 4.0 %collective-permute-start.3 = (f32[128,640]{1,0:T(8,128)S(1)}, f32[128,640]{1,0:T(8,128)S(1)}, u32[]{:S(2)}, u32[]{:S(2)}) collective-permute-start(f32[128,640]{1,0:T(8,128)S(1)} %get-tuple-element.42), channel_id=1, source_target_pairs={{0,4},{1,5},{2,6},{3,7},{4,0},{5,1},{6,2},{7,3},{8,12},{9,13},{10,... | collective-permute-start | bytes 983048 | tf_op jit(solution)/shard_map/ppermute | solution.py:189
  31.1 5.2 %collective-permute-start.6 = (f32[256,128]{1,0:T(8,128)}, f32[256,128]{1,0:T(8,128)S(1)}, u32[]{:S(2)}, u32[]{:S(2)}) collective-permute-start(f32[256,128]{1,0:T(8,128)} %first.1), channel_id=1, source_target_pairs={{0,1},{1,0},{2,3},{3,2},{4,7},{5,6},{6,5},{7,4},{8,9},{9,8},{10,11... | collective-permute-start | bytes 393224 | tf_op jit(solution)/shard_map/ppermute | solution.py:189
  32.8 0.7 %copy-start.1 = (f32[128,640]{1,0:T(8,128)}, f32[128,640]{1,0:T(8,128)S(1)}, u32[]{:S(2)}) copy-start(f32[128,640]{1,0:T(8,128)S(1)} %collective-permute-done.3.other.state) | copy-start | bytes 983044
  33.6 2.8 %copy-start.2 = (f32[256,128]{1,0:T(8,128)S(1)}, f32[256,128]{1,0:T(8,128)}, u32[]{:S(2)}) copy-start(f32[256,128]{1,0:T(8,128)} %first.1) | copy-start | bytes 393220
  36.0 6.0 %copy-start.3 = (f32[256,128]{1,0:T(8,128)S(1)}, f32[256,128]{1,0:T(8,128)}, u32[]{:S(2)}) copy-start(f32[256,128]{1,0:T(8,128)} %second.1) | copy-start | bytes 393220
  36.0 6.0 %collective-permute-start.4 = (f32[256,128]{1,0:T(8,128)}, f32[256,128]{1,0:T(8,128)S(1)}, u32[]{:S(2)}, u32[]{:S(2)}) collective-permute-start(f32[256,128]{1,0:T(8,128)} %second.1), channel_id=1, source_target_pairs={{0,1},{1,0},{2,3},{3,2},{4,7},{5,6},{6,5},{7,4},{8,9},{9,8},{10,11... | collective-permute-start | bytes 393224 | tf_op jit(solution)/shard_map/ppermute | solution.py:189
  36.4 10.4 %collective-permute-start.7 = (f32[256,128]{1,0:T(8,128)S(1)}, f32[256,128]{1,0:T(8,128)S(1)}, u32[]{:S(2)}, u32[]{:S(2)}) collective-permute-start(f32[256,128]{1,0:T(8,128)S(1)} %add.26), channel_id=1, source_target_pairs={{0,3},{1,2},{2,1},{3,0},{4,5},{5,4},{6,7},{7,6},{8,11},{9,10},{10,... | collective-permute-start | bytes 393224 | tf_op jit(solution)/shard_map/ppermute | solution.py:189
  42.0 6.3 %collective-permute-start.5 = (f32[256,128]{1,0:T(8,128)S(1)}, f32[256,128]{1,0:T(8,128)S(1)}, u32[]{:S(2)}, u32[]{:S(2)}) collective-permute-start(f32[256,128]{1,0:T(8,128)S(1)} %add.24), channel_id=1, source_target_pairs={{0,3},{1,2},{2,1},{3,0},{4,5},{5,4},{6,7},{7,6},{8,11},{9,10},{10,... | collective-permute-start | bytes 393224 | tf_op jit(solution)/shard_map/ppermute | solution.py:189
